TPU v7x, 32 devices: a whole 2x2x4 slice. The times are simulated.
32 devices in a mesh: head: 4 (over y, x), tok: 8 (over z, core).
Axes of the slice: x: 2, y: 2, z: 4, core: 2. Of those that a mesh axis runs over, the one named last changes fastest.
Arguments:
- queries: bfloat16 [2, 2048, 5120], P(None, 'tok', 'head'), may hold values from -6 to 6
- key_rows: bfloat16 [2048, 5120], P('tok', 'head'), may hold values from -6 to 6
- value_rows: bfloat16 [2048, 5120], P('tok', 'head'), may hold values from -6 to 6
- step_rates: float32 [20, 2048], P('head', 'tok'), may hold values from 0.05 to 1
- gate_fast: float32 [20, 256, 256], P('head'), may hold values from -0.375 to 0.375
- up_fast: float32 [20, 256, 256], P('head'), may hold values from -0.375 to 0.375
- down_fast: float32 [20, 256, 256], P('head'), may hold values from -0.375 to 0.375
Outputs:
- out_rows: bfloat16 [2, 2048, 5120], P(None, ('tok', 'head'))
All inputs are finite; a program needn't handle non-finite values.
Results may differ from a plain program's by a relative error of at most 0.011.
Values may be sent and summed in bfloat16 or wider, within the bound.
A program may use at most 64 MiB of HBM per device.

v0:
```python
import functools

import jax
import jax.numpy as jnp
from jax import lax
from jax.experimental import pallas as pl
from jax.experimental.pallas import tpu as pltpu
from jax.sharding import PartitionSpec as P

NS_STEPS = 3
KINDS = 3
PIECES = 2
EXTRA = 2
DEPTH = 4

coef_first = 3.4445
coef_second = -4.775
coef_third = 2.0315

MESH = pl.DeviceIdType.MESH
BF = jnp.bfloat16
F32 = jnp.float32


def mm(a, b):
    return jnp.dot(a, b, preferred_element_type=F32)


def mm_tn(a, b):
    return lax.dot_general(a, b, (((0,), (0,)), ((), ())), preferred_element_type=F32)


def mm_nt(a, b):
    return lax.dot_general(a, b, (((1,), (1,)), ((), ())), preferred_element_type=F32)


def fast_apply(x, gate, up, down):
    pre = mm(x, gate)
    hidden = (pre / (1.0 + jnp.exp(-pre)) * mm(x, up)).astype(BF)
    return mm(hidden, down).astype(BF)


def kernel(
    nh, nz, q_in, k_in, v_in, rates, g_in, u_in, d_in, out,
    qb, kb, vb, wf, wh, gb, pb, cs, cr, wn, ob,
    in_sem, ps_s, ps_r, ch_s, ch_r, ag_s, ag_r, ap_s, ap_r, a_s, a_r, a_l,
):
    heads, rows, size = kb.shape
    count = KINDS * heads
    pairs = pb.shape[0]
    piece = size // PIECES
    share = rows // nh
    hd = lax.axis_index("head")
    tok = lax.axis_index("tok")
    lane = lax.rem(tok, 2)
    z = tok // 2
    partner = (hd, z * 2 + 1 - lane)

    def cut(h):
        return pl.ds(h * size if isinstance(h, int) else pl.multiple_of(h * size, size), size)

    def load(at, h):
        src, dst = (
            (k_in.at[:, cut(h)], kb.at[h]),
            (g_in.at[h], wf.at[0, h]),
            (u_in.at[h], wf.at[1, h]),
            (v_in.at[:, cut(h)], vb.at[h]),
            (d_in.at[h], wf.at[2, h]),
            (q_in.at[0, :, cut(h)], qb.at[0, h]),
            (q_in.at[1, :, cut(h)], qb.at[1, h]),
        )[at]
        return pltpu.make_async_copy(src, dst, in_sem.at[at, h])

    for h in range(heads):
        for at in range(5):
            load(at, h).start()
    for h in range(heads):
        for at in (5, 6):
            load(at, h).start()

    barrier = pltpu.get_barrier_semaphore()
    pl.semaphore_signal(barrier, inc=1, device_id=partner, device_id_type=MESH)
    for p in range(1, nh):
        pl.semaphore_signal(
            barrier, inc=1, device_id=(lax.rem(hd + p, nh), tok), device_id_type=MESH
        )

    @pl.when(z > 0)
    def _():
        pl.semaphore_signal(barrier, inc=1, device_id=(hd, tok - 2), device_id_type=MESH)

    @pl.when(z < nz - 1)
    def _():
        pl.semaphore_signal(barrier, inc=1, device_id=(hd, tok + 2), device_id_type=MESH)

    inner = (z > 0).astype(jnp.int32) + (z < nz - 1).astype(jnp.int32)
    pl.semaphore_wait(barrier, nh + inner)

    def mine(j):
        return 2 * j + lane

    def side(j):
        return lax.rem(j, 2)

    def is_start(j):
        return z == (1 - side(j)) * (nz - 1)

    def is_owner(j):
        return z == side(j) * (nz - 1)

    def towards(j):
        return (hd, tok + (2 * side(j) - 1) * 2)

    def back(j):
        return (hd, tok - (2 * side(j) - 1) * 2)

    def swap(j):
        return pltpu.make_async_remote_copy(
            gb.at[2 * j + 1 - lane], pb.at[j], ps_s.at[j], ps_r.at[j],
            device_id=partner, device_id_type=MESH,
        )

    def chain(j, g):
        part = pl.ds(g * piece, piece)
        return pltpu.make_async_remote_copy(
            cs.at[j, part], cr.at[j, part], ch_s.at[j, g], ch_r.at[j, g],
            device_id=towards(j), device_id_type=MESH,
        )

    def spread(j, g):
        part = pl.ds(g * piece, piece)
        return pltpu.make_async_remote_copy(
            wn.at[mine(j), part], wn.at[mine(j), part], ag_s.at[j, g], ag_r.at[j, g],
            device_id=back(j), device_id_type=MESH,
        )

    def across(j, g, m):
        part = pl.ds(g * piece, piece)
        return pltpu.make_async_remote_copy(
            wn.at[m, part], wn.at[m, part], ap_s.at[j, g], ap_r.at[j, g],
            device_id=partner, device_id_type=MESH,
        )

    def launch(make, j, g):
        before = j + 2 * ((g - DEPTH) // PIECES)

        @pl.when(before >= 0)
        def _():
            make(before, (g - DEPTH) % PIECES).wait_send()

        make(j, g).start()

    def land(make, j, g):
        @pl.when(mine(j + 2 * ((g + DEPTH) // PIECES)) >= count)
        def _():
            make(j, g).wait_send()

    def wide(h):
        return pl.ds(pl.multiple_of((hd * heads + h) * size, size), size)

    def deal(b, h, p):
        peer = lax.rem(hd + p, nh)
        return pltpu.make_async_remote_copy(
            ob.at[b, h, pl.ds(pl.multiple_of(peer * share, share), share)],
            out.at[b, :, wide(h)],
            a_s.at[b, h, p - 1], a_r.at[b, h, p - 1],
            device_id=(peer, tok), device_id_type=MESH,
        )

    def arrive(b, h, p):
        source = lax.rem(hd + nh - p, nh)
        return pltpu.make_async_remote_copy(
            ob.at[b, h, pl.ds(pl.multiple_of(hd * share, share), share)],
            out.at[b, :, pl.ds(pl.multiple_of((source * heads + h) * size, size), size)],
            a_s.at[b, h, p - 1], a_r.at[b, h, p - 1],
            device_id=(source, tok), device_id_type=MESH,
        )

    def keep(b, h):
        return pltpu.make_async_copy(
            ob.at[b, h, pl.ds(pl.multiple_of(hd * share, share), share)],
            out.at[b, :, wide(h)], a_l.at[b, h],
        )

    def deal_all(b, h):
        for p in range(nh - 1, 0, -1):
            deal(b, h, p).start()
        keep(b, h).start()

    def wait_load(h, picks):
        for at in picks:
            load(at, h).wait()

    def gradients(h):
        wait_load(h, range(5))
        keys = kb[h]
        gate = wf[0, h].astype(BF)
        up = wf[1, h].astype(BF)
        down = wf[2, h].astype(BF)
        wh[0, h] = gate
        wh[1, h] = up
        wh[2, h] = down
        zg = mm(keys, gate)
        zu = mm(keys, up)
        sig = 1.0 / (1.0 + jnp.exp(-zg))
        silu = zg * sig
        hidden = (silu * zu).astype(BF)
        line = jnp.broadcast_to(rates[pl.ds(h, 1), :], (128, rows))
        column = jnp.transpose(line)
        column = jnp.concatenate([column] * (size // 128), axis=1)
        dout = (-(column * vb[h].astype(F32))).astype(BF)
        dh = mm_nt(dout, down)
        dzu = (dh * silu).astype(BF)
        dzg = (dh * zu * sig * (1.0 + zg * (1.0 - sig))).astype(BF)
        base = KINDS * h
        gb[base] = mm_tn(keys, dzg).astype(BF)
        gb[base + 1] = mm_tn(keys, dzu).astype(BF)
        gb[base + 2] = mm_tn(hidden, dout).astype(BF)
        for kind in range(KINDS):
            m = base + kind

            @pl.when(lax.rem(m, 2) != lane)
            def _():
                swap(m // 2).start()

    def first(h):
        wait_load(h, (5,))
        ob[0, h] = fast_apply(qb[0, h], wh[0, h], wh[1, h], wh[2, h])
        deal_all(0, h)

    def own(h, step):
        for kind in range(KINDS):
            m = KINDS * h + kind

            @pl.when(lax.rem(m, 2) == lane)
            def _():
                step(m // 2)

    def start_step(j):
        swap(j).wait_recv()

        @pl.when(is_start(j))
        def _():
            cs[j] = (gb[mine(j)].astype(F32) + pb[j].astype(F32)).astype(BF)
            for g in range(PIECES):
                launch(chain, j, g)

    def pass_step(j):
        @pl.when(jnp.logical_not(is_start(j)) & jnp.logical_not(is_owner(j)))
        def _():
            for g in range(PIECES):
                part = pl.ds(g * piece, piece)
                chain(j, g).wait_recv()
                cs[j, part] = (
                    gb[mine(j), part].astype(F32)
                    + pb[j, part].astype(F32)
                    + cr[j, part].astype(F32)
                ).astype(BF)
                launch(chain, j, g)

    lag = EXTRA + max(
        min((2 * j + 1) // KINDS, heads - 1) + 1 - (j // 2 + 1) for j in range(pairs)
    )
    turns = (pairs - 1) // 2 + nz - 1
    total = max(2 * heads, turns + lag)

    def reach(j):
        return jnp.where(side(j) == 0, nz - 1 - z, z)

    @pl.loop(0, total)
    def _(t):
        @pl.when(t < heads)
        def _():
            gradients(t)

        @pl.when((t >= heads) & (t < 2 * heads))
        def _():
            first(t - heads)

        @pl.when((t >= 1) & (t <= heads))
        def _():
            own(t - 1, start_step)

        for s in range(2):
            i = t - lag - reach(s)
            j = 2 * i + s

            @pl.when((i >= 0) & (j < pairs) & (mine(j) < count))
            def _():
                pass_step(j)

    @pl.loop(0, pairs)
    def _(j):
        m = mine(j)

        @pl.when((m < count) & is_owner(j))
        def _():
            for g in range(PIECES):
                chain(j, g).wait_recv()
            grad = gb[m].astype(F32) + pb[j].astype(F32) + cr[j].astype(F32)
            scale = jnp.sqrt(jnp.sum(grad * grad)) + 1e-07
            x = grad / scale
            for _ in range(NS_STEPS):
                xb = x.astype(BF)
                gram = mm_tn(xb, xb)
                half = gram.astype(BF)
                poly = coef_second * gram + coef_third * mm(half, half)
                x = coef_first * x + mm(xb, poly.astype(BF))
            wn[m] = (wf[lax.rem(m, KINDS), m // KINDS] - x).astype(BF)
            for g in range(PIECES):
                launch(spread, j, g)
                across(j, g, m).start()

    def second(h):
        for kind in range(KINDS):
            m = KINDS * h + kind

            @pl.when(lax.rem(m, 2) != lane)
            def _():
                for g in range(PIECES):
                    across(m // 2, g, m).wait_recv()

        wait_load(h, (6,))
        base = KINDS * h
        ob[1, h] = fast_apply(qb[1, h], wn[base], wn[base + 1], wn[base + 2])
        deal_all(1, h)

    def relay(j):
        m = mine(j)
        for g in range(PIECES):
            spread(j, g).wait_recv()

            @pl.when(jnp.logical_not(is_start(j)))
            def _():
                launch(spread, j, g)

            across(j, g, m).start()

    def away(j):
        return jnp.where(side(j) == 0, z, nz - 1 - z)

    @pl.loop(0, (pairs - 1) // 2 + nz)
    def _(t):
        for s in range(2):
            i = t - away(s)
            j = 2 * i + s

            @pl.when((i >= 0) & (j < pairs) & (mine(j) < count) & jnp.logical_not(is_owner(j)))
            def _():
                relay(j)

        @pl.loop(0, heads)
        def _(h):
            top = (KINDS * h + KINDS - 1) // 2
            below = top - 1
            due = jnp.maximum(top // 2 + away(top), below // 2 + away(below))

            @pl.when(due == t)
            def _():
                second(h)

    @pl.loop(0, pairs)
    def _(j):
        m = mine(j)

        @pl.when(2 * j + 1 - lane < count)
        def _():
            swap(j).wait_send()

        @pl.when(m < count)
        def _():
            for g in range(PIECES):
                across(j, g, m).wait_send()

                @pl.when(jnp.logical_not(is_owner(j)))
                def _():
                    land(chain, j, g)

                @pl.when(jnp.logical_not(is_start(j)))
                def _():
                    land(spread, j, g)

    for b in range(2):
        @pl.loop(0, heads)
        def _(h):
            for p in range(1, nh):
                arrive(b, h, p).wait_recv()
                deal(b, h, p).wait_send()
            keep(b, h).wait()


def solution(mesh):
    nh = mesh.shape["head"]
    nz = mesh.shape["tok"] // 2

    def local(queries, key_rows, value_rows, step_rates, gate_fast, up_fast, down_fast):
        heads, size, _ = gate_fast.shape
        rows = key_rows.shape[0]
        pairs = (KINDS * heads + 1) // 2
        anywhere = pl.BlockSpec(memory_space=pl.ANY)
        dma = pltpu.SemaphoreType.DMA
        return pl.pallas_call(
            functools.partial(kernel, nh, nz),
            out_shape=jax.ShapeDtypeStruct((2, rows // nh, nh * heads * size), BF),
            in_specs=[
                anywhere, anywhere, anywhere,
                pl.BlockSpec(memory_space=pltpu.VMEM),
                anywhere, anywhere, anywhere,
            ],
            out_specs=anywhere,
            scratch_shapes=[
                pltpu.VMEM((2, heads, rows, size), BF),
                pltpu.VMEM((heads, rows, size), BF),
                pltpu.VMEM((heads, rows, size), BF),
                pltpu.VMEM((KINDS, heads, size, size), F32),
                pltpu.VMEM((KINDS, heads, size, size), BF),
                pltpu.VMEM((2 * pairs, size, size), BF),
                pltpu.VMEM((pairs, size, size), BF),
                pltpu.VMEM((pairs, size, size), BF),
                pltpu.VMEM((pairs, size, size), BF),
                pltpu.VMEM((2 * pairs, size, size), BF),
                pltpu.VMEM((2, heads, rows, size), BF),
                dma((7, heads)),
                dma((pairs,)), dma((pairs,)),
                dma((pairs, PIECES)), dma((pairs, PIECES)),
                dma((pairs, PIECES)), dma((pairs, PIECES)),
                dma((pairs, PIECES)), dma((pairs, PIECES)),
                dma((2, heads, nh - 1)), dma((2, heads, nh - 1)),
                dma((2, heads)),
            ],
            compiler_params=pltpu.CompilerParams(
                collective_id=0, has_side_effects=True, vmem_limit_bytes=67043328
            ),
        )(queries, key_rows, value_rows, step_rates, gate_fast, up_fast, down_fast)

    placed = (
        P(None, "tok", "head"),
        P("tok", "head"),
        P("tok", "head"),
        P("head", "tok"),
        P("head", None, None),
        P("head", None, None),
        P("head", None, None),
    )
    return jax.shard_map(
        local, mesh=mesh, in_specs=placed, out_specs=P(None, ("tok", "head"), None), check_vma=False
    )
```

profile of v0, /device:TPU:0, one launch (start us, length us, event | category | flops | bytes accessed | tf_op | source)
XLA Modules:
  0.0 53.0 jit_solution(1849870849797316291)
XLA Ops:
  0.0 50.6 %shard_map.73 = bf16[2,64,5120]{2,1,0:T(8,128)(2,1)} custom-call(bf16[2,256,1280]{2,1,0:T(8,128)(2,1)} %q_in.1, bf16[256,1280]{1,0:T(8,128)(2,1)} %k_in.1, bf16[256,1280]{1,0:T(8,128)(2,1)} %v_in.1, f32[5,256]{1,0:T(8,128)} %rates.1, f32[5,256,256]{2,1,0:T(8,128)} %g_in.1, f32[5,256,256]{2,1,0:T(8,128)} %u_in.1, f32[5,256,256]{2,1,0:T(8,128)} %d_in.1), custom_call_target="tpu_custom_call" | custom-call | tf_op jit(solution)/shard_map/pallas_call | solution.py:402
  50.6 2.5 %copy.9 = bf16[2,64,5120]{2,1,0:T(8,128)(2,1)} copy(bf16[2,64,5120]{2,1,0:T(8,128)(2,1)} %shard_map.73) | data formatting | bytes 2621440
where the time goes:
time: 53.2 us; the launch traced here: 53 us
  Pallas kernels  50.6 us (95%)
  local copies, waits for them, and re-layouts  2.46 us (5%)
    pallas_call x1, Pallas kernels, local(): pl.pallas_call(functools.partial(kernel, nh, nz), out_shape=jax.ShapeDtyp...  50.6 us
    unnamed x1, local copies, waits for them, and re-layouts  2.46 us

commit v1 on v0

--- a/solution.py
+++ b/solution.py
@@ -401,13 +401,13 @@
         dma = pltpu.SemaphoreType.DMA
         return pl.pallas_call(
             functools.partial(kernel, nh, nz),
-            out_shape=jax.ShapeDtypeStruct((2, rows // nh, nh * heads * size), BF),
+            out_shape=pltpu.VMEM((2, rows // nh, nh * heads * size), BF),
             in_specs=[
                 anywhere, anywhere, anywhere,
                 pl.BlockSpec(memory_space=pltpu.VMEM),
                 anywhere, anywhere, anywhere,
             ],
-            out_specs=anywhere,
+            out_specs=pl.BlockSpec(memory_space=pltpu.VMEM),
             scratch_shapes=[
                 pltpu.VMEM((2, heads, rows, size), BF),
                 pltpu.VMEM((heads, rows, size), BF),
@@ -429,7 +429,7 @@
                 dma((2, heads)),
             ],
             compiler_params=pltpu.CompilerParams(
-                collective_id=0, has_side_effects=True, vmem_limit_bytes=67043328
+                collective_id=0, has_side_effects=True, vmem_limit_bytes=67043328-1310720-16384
             ),
         )(queries, key_rows, value_rows, step_rates, gate_fast, up_fast, down_fast)
 

time: 53.2 us -> 51.6 us (0.970)
  local copies, waits for them, and re-layouts: 2.46 us -> 1.06 us
    unnamed x1, local copies, waits for them, and re-layouts: 2.46 us -> 1.06 us
where the time goes in v1:
time: 51.6 us; the launch traced here: 51.4 us
  Pallas kernels  50.3 us (97%)
  local copies, waits for them, and re-layouts  1.06 us (2%)
    pallas_call x1, Pallas kernels, local(): pl.pallas_call(functools.partial(kernel, nh, nz), out_shape=pltpu.VMEM((2...  50.3 us
    unnamed x1, local copies, waits for them, and re-layouts  1.06 us

profile of v1, /device:TPU:0, one launch (start us, length us, event | category | flops | bytes accessed | tf_op | source)
XLA Modules:
  0.0 51.4 jit_solution(7704775062319907732)
XLA Ops:
  0.0 50.3 %shard_map.73 = bf16[2,64,5120]{2,1,0:T(8,128)(2,1)S(1)} custom-call(bf16[2,256,1280]{2,1,0:T(8,128)(2,1)} %q_in.1, bf16[256,1280]{1,0:T(8,128)(2,1)} %k_in.1, bf16[256,1280]{1,0:T(8,128)(2,1)} %v_in.1, f32[5,256]{1,0:T(8,128)} %rates.1, f32[5,256,256]{2,1,0:T(8,128)} %g_in.1, f32[5,256,256]{2,1,0:T(8,128)} %u_in.1, f32[5,256,256]{2,1,0:T(8,128)} %d_in.1), custom_call_target="tpu_custom_call" | custom-call | tf_op jit(solution)/shard_map/pallas_call | solution.py:402
  50.3 1.1 %copy.9 = bf16[2,64,5120]{2,1,0:T(8,128)(2,1)} copy(bf16[2,64,5120]{2,1,0:T(8,128)(2,1)S(1)} %shard_map.73) | data formatting | bytes 2621440

commit v2 on v1

v2 whole, which is shorter than its diff:
```python
import functools

import jax
import jax.numpy as jnp
from jax import lax
from jax.experimental import pallas as pl
from jax.experimental.pallas import tpu as pltpu
from jax.sharding import PartitionSpec as P

NS_STEPS = 3
KINDS = 3
PIECES = 4
LAG = 5
LAG_ALONE = 9
VMEM_BYTES = 67043328

coef_first = 3.4445
coef_second = -4.775
coef_third = 2.0315

MESH = pl.DeviceIdType.MESH
BF = jnp.bfloat16
F32 = jnp.float32


def mm(a, b):
    return jnp.dot(a, b, preferred_element_type=F32)


def mm_tn(a, b):
    return lax.dot_general(a, b, (((0,), (0,)), ((), ())), preferred_element_type=F32)


def mm_nt(a, b):
    return lax.dot_general(a, b, (((1,), (1,)), ((), ())), preferred_element_type=F32)


def fast_apply(x, gate, up, down):
    pre = mm(x, gate)
    hidden = (pre / (1.0 + jnp.exp(-pre)) * mm(x, up)).astype(BF)
    return mm(hidden, down).astype(BF)


def kernel(
    nh, nz, q_in, k_in, v_in, r_in, g_in, u_in, d_in, out,
    qb, qn, kb, vb, rb, wf, wh, own, sent, got, pi, si, po, so, mg, xs, gm, pm, wn, ob, ox,
    ld, qs, sw_s, sw_r, p_s, p_r, s_s, s_r, a_s, a_r, b_s, b_r, b_p, b_l,
):
    heads, share, size = ob.shape[0], ob.shape[1] // nh, ob.shape[2]
    rows = nh * share
    slots = sent.shape[0]
    piece = size // PIECES
    per = KINDS * PIECES
    hd = lax.axis_index("head")
    tok = lax.axis_index("tok")
    lane = lax.rem(tok, 2)
    z = tok // 2
    partner = (hd, z * 2 + 1 - lane)
    total = per * ((heads + 1 - lane) // 2)
    first_end = z == 0
    last_end = z == nz - 1
    middle = jnp.logical_not(first_end) & jnp.logical_not(last_end)

    def cut(h):
        return pl.ds(h * size if isinstance(h, int) else pl.multiple_of(h * size, size), size)

    def mine(i):
        return 2 * i + lane

    def theirs(i):
        return 2 * i + 1 - lane

    barrier = pltpu.get_barrier_semaphore()

    @pl.when(z > 0)
    def _():
        pl.semaphore_signal(barrier, inc=1, device_id=(hd, tok - 2), device_id_type=MESH)

    @pl.when(z < nz - 1)
    def _():
        pl.semaphore_signal(barrier, inc=1, device_id=(hd, tok + 2), device_id_type=MESH)

    pl.semaphore_signal(barrier, inc=1, device_id=partner, device_id_type=MESH)
    for p in range(1, nh):
        for c in range(2):
            pl.semaphore_signal(
                barrier, inc=1, device_id=(lax.rem(hd + p, nh), 2 * z + c), device_id_type=MESH
            )
    inner = (z > 0).astype(jnp.int32) + (z < nz - 1).astype(jnp.int32)

    def load_head(stage, columns, some):
        pltpu.make_async_copy(k_in.at[:, columns], kb.at[:, columns], ld.at[stage, 0]).start()
        for k, src in enumerate((g_in, u_in)):
            pltpu.make_async_copy(src.at[some], wf.at[k, some], ld.at[stage, 1]).start()
        pltpu.make_async_copy(v_in.at[:, columns], vb.at[:, columns], ld.at[stage, 0]).start()
        pltpu.make_async_copy(d_in.at[some], wf.at[2, some], ld.at[stage, 1]).start()

    def wait_head(stage, count):
        both = q_in.at[:, :, pl.ds(0, count * size)]
        pltpu.make_async_copy(both, both, ld.at[stage, 0]).wait()
        three = wf.at[:, pl.ds(0, count)]
        pltpu.make_async_copy(three, three, ld.at[stage, 1]).wait()

    load_rates = pltpu.make_async_copy(r_in, rb, ld.at[3, 0])
    load_first = pltpu.make_async_copy(q_in.at[0], qb, ld.at[3, 1])
    load_next = pltpu.make_async_copy(q_in.at[1], qn.at[lane], ld.at[4, 0])
    push_next = pltpu.make_async_remote_copy(
        q_in.at[1], qn.at[lane], qs.at[0], qs.at[1], device_id=partner, device_id_type=MESH
    )

    def place(t):
        return t // PIECES, pl.ds(pl.multiple_of(lax.rem(t, PIECES) * piece, piece), piece)

    def right(src, t):
        m, part = place(t)
        return pltpu.make_async_remote_copy(
            src.at[m, part], pi.at[m, part], p_s.at[t // per], p_r.at[t],
            device_id=(hd, tok + 2), device_id_type=MESH,
        )

    def left(src, t):
        m, part = place(t)
        return pltpu.make_async_remote_copy(
            src.at[m, part], si.at[m, part], s_s.at[t // per], s_r.at[t],
            device_id=(hd, tok - 2), device_id_type=MESH,
        )

    def swap(i, k):
        return pltpu.make_async_remote_copy(
            sent.at[i, k], got.at[i, k], sw_s.at[i], sw_r.at[i, k],
            device_id=partner, device_id_type=MESH,
        )

    def wide(h):
        return pl.ds(pl.multiple_of((hd * heads + h) * size, size), size)

    def band(peer):
        return pl.ds(pl.multiple_of(peer * share, share), share)

    order = (3, 1, 2, 0) if nh == 4 else tuple(range(nh - 1, -1, -1))

    def other(p):
        if nh != 4 or p == 0:
            return lax.rem(hd + p, nh)
        return (hd + 1 - 2 * lax.rem(hd, 2), lax.rem(hd + 2, 4), 3 - hd)[p - 1]

    def deal(h, p):
        peer = other(p)
        return pltpu.make_async_remote_copy(
            ob.at[h, band(peer)], out.at[0, :, wide(h)], a_s.at[0], a_r.at[p - 1],
            device_id=(peer, tok), device_id_type=MESH,
        )

    def keep(h):
        return pltpu.make_async_copy(ob.at[h, band(hd)], out.at[0, :, wide(h)], a_s.at[1])

    def deal_next(i, c, p):
        peer = other(p)
        return pltpu.make_async_remote_copy(
            ox.at[i, c * nh + peer], out.at[1, :, wide(mine(i))],
            b_s.at[i], b_p.at[i] if p == 0 else b_r.at[p - 1],
            device_id=(peer, 2 * z + c), device_id_type=MESH,
        )

    def keep_next(i):
        return pltpu.make_async_copy(
            ox.at[i, lane * nh + hd], out.at[1, :, wide(mine(i))], b_l.at[i]
        )

    def gradients(h):
        keys = kb[:, cut(h)]
        gate = wf[0, h].astype(BF)
        up = wf[1, h].astype(BF)
        down = wf[2, h].astype(BF)
        wh[0, h] = gate
        wh[1, h] = up
        wh[2, h] = down
        zg = mm(keys, gate)
        zu = mm(keys, up)
        sig = 1.0 / (1.0 + jnp.exp(-zg))
        silu = zg * sig
        hidden = (silu * zu).astype(BF)
        line = jnp.broadcast_to(rb[pl.ds(h, 1), :], (128, rows))
        column = jnp.transpose(line)
        column = jnp.concatenate([column] * (size // 128), axis=1)
        dout = (-(column * vb[:, cut(h)].astype(F32))).astype(BF)
        dh = mm_nt(dout, down)
        dzu = (dh * silu).astype(BF)
        dzg = (dh * zu * sig * (1.0 + zg * (1.0 - sig))).astype(BF)
        return mm_tn(keys, dzg), mm_tn(keys, dzu), mm_tn(hidden, dout)

    def gradients_theirs(i):
        parts = gradients(theirs(i))
        for k in range(KINDS):
            sent[i, k] = parts[k].astype(BF)

    def gradients_mine(i):
        parts = gradients(mine(i))
        for k in range(KINDS):
            mg[k] = parts[k]

    def add_theirs(i):
        for k in range(KINDS):
            swap(i, k).wait_recv()
            own[KINDS * i + k] = (mg[k] + got[i, k].astype(F32)).astype(BF)

            @pl.when(first_end)
            def _():
                for g in range(PIECES):
                    right(own, per * i + k * PIECES + g).start()

            @pl.when(last_end)
            def _():
                for g in range(PIECES):
                    left(own, per * i + k * PIECES + g).start()

    turn_at = per * (slots - 1)
    alone = (mine(slots - 1) < heads) & (theirs(slots - 1) >= heads)

    def turn(t, far):
        fast = (LAG_ALONE - LAG) * far
        held = jnp.where(t < turn_at + fast, -1, t - LAG_ALONE * far)
        return jnp.where(alone & (t >= turn_at), held, t - LAG * far)

    def pass_on(t):
        p = turn(t, z - 1)
        s = turn(t, nz - 2 - z)

        @pl.when(middle & (p >= 0) & (p < total))
        def _():
            m, part = place(p)
            right(po, p).wait_recv()
            po[m, part] = (pi[m, part].astype(F32) + own[m, part].astype(F32)).astype(BF)
            right(po, p).start()

        @pl.when(middle & (s >= 0) & (s < total))
        def _():
            m, part = place(s)
            left(so, s).wait_recv()
            so[m, part] = (si[m, part].astype(F32) + own[m, part].astype(F32)).astype(BF)
            left(so, s).start()

    def first(h):
        ob[h] = fast_apply(qb[:, cut(h)], wh[0, h], wh[1, h], wh[2, h])
        for p in order[:-1]:
            deal(h, p).start()
        keep(h).start()

    def gather_some(i, kinds):
        for k in kinds:
            m = KINDS * i + k

            @pl.when(first_end)
            def _():
                for g in range(PIECES):
                    left(own, per * i + k * PIECES + g).wait_recv()
                xs[k] = own[m].astype(F32) + si[m].astype(F32)

            @pl.when(last_end)
            def _():
                for g in range(PIECES):
                    right(own, per * i + k * PIECES + g).wait_recv()
                xs[k] = own[m].astype(F32) + pi[m].astype(F32)

            @pl.when(middle)
            def _():
                xs[k] = own[m].astype(F32) + pi[m].astype(F32) + si[m].astype(F32)

        grads = [xs[k] for k in kinds]
        scales = [1.0 / (jnp.sqrt(jnp.sum(v * v)) + 1e-07) for v in grads]
        for k, v, scale in zip(kinds, grads, scales):
            xs[k] = v * scale

    def gather(i):
        gather_some(i, range(KINDS - 1))
        gather_some(i, [KINDS - 1])

    def gram_all():
        for k in range(KINDS):
            x = xs[k].astype(BF)
            gm[k] = mm_nt(x, x)

    def poly_all():
        for k in range(KINDS):
            half = gm[k].astype(BF)
            pm[k] = (coef_second * gm[k] + coef_third * mm(half, half)).astype(BF)

    def apply_all():
        for k in range(KINDS):
            xs[k] = coef_first * xs[k] + mm(pm[k], xs[k].astype(BF))

    def sweep():
        x = [xs[k] for k in range(KINDS)]
        xb = [v.astype(BF) for v in x]
        gram = [mm_nt(v, v) for v in xb]
        half = [v.astype(BF) for v in gram]
        square = [mm(v, v) for v in half]
        poly = [(coef_second * a + coef_third * b).astype(BF) for a, b in zip(gram, square)]
        for k in range(KINDS):
            xs[k] = coef_first * x[k] + mm(poly[k], xb[k])

    def update(i):
        for k in range(KINDS):
            wn[k] = (wf[k, mine(i)] - xs[k]).astype(BF)

    def second(i):
        x = qn[:, :, cut(mine(i))].reshape(2 * rows, size)
        ox[i] = fast_apply(x, wn[0], wn[1], wn[2]).reshape(2 * nh, share, size)
        for p in order:
            for c in range(2):
                if p > 0:
                    deal_next(i, c, p).start()
                else:

                    @pl.when(lane != c)
                    def _():
                        deal_next(i, c, p).start()

        keep_next(i).start()

    def ready_theirs(i):
        @pl.when(theirs(i) < heads)
        def _():
            gradients_theirs(i)
            for k in range(KINDS):
                swap(i, k).start()

    def add_mine(i):
        @pl.when(mine(i) < heads)
        def _():
            add_theirs(i)

    def ready_mine(i):
        @pl.when((i < slots) & (mine(i) < heads))
        def _():
            gradients_mine(i)
            add_theirs(i)

    def first_of(h):
        @pl.when(h < heads)
        def _():
            first(h)

    load_rates.start()
    load_head(0, cut(theirs(0)), pl.ds(theirs(0), 1))
    load_head(1, cut(mine(0)), pl.ds(mine(0), 1))
    load_rates.wait()
    wait_head(0, 1)
    if heads > 2:
        rest = heads - 2
        load_head(2, pl.ds(2 * size, rest * size), pl.ds(2, rest))
    load_first.start()
    load_next.start()
    gradients_theirs(0)
    wait_head(1, 1)
    gradients_mine(0)
    pl.semaphore_wait(barrier, 1 + 2 * (nh - 1) + inner)
    for k in range(KINDS):
        swap(0, k).start()
    add_theirs(0)
    if heads > 2:
        wait_head(2, rest)

        @pl.loop(1, slots)
        def _(i):
            ready_theirs(i)

    push_next.start()
    if slots > 1:

        @pl.when(mine(1) < heads)
        def _():
            gradients_mine(1)

    hops = max(nz - 3, 0)
    late = LAG * hops if turn_at - LAG * hops >= per * (slots - 2) else LAG_ALONE * hops
    behind, offset = late // per, late % per
    defer = middle & (mine(slots - 1) < heads)

    def finish(i):
        update(i)
        second(i)

    load_first.wait()

    @pl.loop(0, slots + behind)
    def _(r):
        base = per * r
        i = r - 1 - behind

        def done(work):
            def run():
                @pl.when((i >= 0) & jnp.logical_not(defer & (i == slots - 2)))
                def _():
                    work()

            return run

        def begin():
            @pl.when(i == 0)
            def _():
                load_next.wait()
                push_next.wait_recv()

            gather(i)

        start = offset
        work = {1: [lambda: ready_mine(r + 2)]}
        firsts = (heads + 1) // 2
        for n in range(firsts):
            work[2 * n + 3] = [lambda n=n: first_of(firsts * r + n)]
        tail = []
        for n, item in enumerate([begin, None, sweep, sweep, None, sweep, lambda: finish(i)]):
            if item is None:
                continue
            if start + n < per:
                work.setdefault(start + n, []).append(done(item))
            else:
                tail.append(done(item))
        for t in range(per):
            pass_on(base + t)
            if t == 0 and slots > 1:

                @pl.when(r == 0)
                def _():
                    add_mine(1)

            for item in work.get(t, []):
                item()
        for item in tail:
            item()

    def last_wait(i):
        if slots <= 2:

            @pl.when(i == 0)
            def _():
                load_next.wait()
                push_next.wait_recv()

    begun = per * (slots + behind)
    ended = per * slots + LAG_ALONE * hops
    held = max(slots - 2, 0)
    small = [lambda k=k: gather_some(held, [k]) for k in range(KINDS)]
    small += [gram_all, poly_all, apply_all] * NS_STEPS
    if nz == 4 and slots > 1:
        for t in range(begun, ended):
            pass_on(t)

            @pl.when(defer)
            def _():
                if t == begun:
                    last_wait(held)
                n = t - begun
                for run in small[n * len(small) // (ended - begun) : (n + 1) * len(small) // (ended - begun)]:
                    run()
    else:

        @pl.loop(begun, ended)
        def _(t):
            pass_on(t)

        @pl.when(defer)
        def _():
            last_wait(held)
            for run in small:
                run()

    @pl.when(defer)
    def _():
        if slots > 1:
            finish(held)

    @pl.when(mine(slots - 1) < heads)
    def _():
        if slots == 1:
            last_wait(0)
        gather(slots - 1)
        for s in range(NS_STEPS):
            sweep()
        finish(slots - 1)

    push_next.wait_send()

    @pl.loop(0, slots)
    def _(i):
        @pl.when(theirs(i) < heads)
        def _():
            pltpu.make_async_copy(sent.at[i], sent.at[i], sw_s.at[i]).wait()
            part = ox.at[i, 0]
            pltpu.make_async_copy(part, part, b_p.at[i]).wait()

        @pl.when(mine(i) < heads)
        def _():
            part = ox.at[i, pl.ds(0, 2 * nh - 1)]
            pltpu.make_async_copy(part, part, b_s.at[i]).wait()
            keep_next(i).wait()
            slot = own.at[pl.ds(KINDS * i, KINDS)]

            @pl.when(z < nz - 1)
            def _():
                pltpu.make_async_copy(slot, slot, p_s.at[i]).wait()

            @pl.when(z > 0)
            def _():
                pltpu.make_async_copy(slot, slot, s_s.at[i]).wait()

    part = ob.at[:, pl.ds(0, (nh - 1) * share)]
    pltpu.make_async_copy(part, part, a_s.at[0]).wait()
    part = ob.at[:, pl.ds(0, share)]
    pltpu.make_async_copy(part, part, a_s.at[1]).wait()
    for p in range(1, nh):
        part = out.at[0, :, pl.ds(0, heads * size)]
        pltpu.make_async_copy(part, part, a_r.at[p - 1]).wait()
        part = out.at[1, :, pl.ds(0, heads * size)]
        pltpu.make_async_copy(part, part, b_r.at[p - 1]).wait()


def solution(mesh):
    nh = mesh.shape["head"]
    nz = mesh.shape["tok"] // 2

    def local(queries, key_rows, value_rows, step_rates, gate_fast, up_fast, down_fast):
        heads, size, _ = gate_fast.shape
        rows = key_rows.shape[0]
        slots = (heads + 1) // 2
        matrices = KINDS * slots
        pieces = matrices * PIECES
        out_shape = (2, rows // nh, nh * heads * size)
        out_bytes = 2 * out_shape[0] * out_shape[1] * out_shape[2]
        anywhere = pl.BlockSpec(memory_space=pl.ANY)
        dma = pltpu.SemaphoreType.DMA
        stack = pltpu.VMEM((matrices, size, size), BF)
        return pl.pallas_call(
            functools.partial(kernel, nh, nz),
            out_shape=pltpu.VMEM(out_shape, BF),
            in_specs=[anywhere] * 7,
            out_specs=pl.BlockSpec(memory_space=pltpu.VMEM),
            scratch_shapes=[
                pltpu.VMEM((rows, heads * size), BF),
                pltpu.VMEM((2, rows, heads * size), BF),
                pltpu.VMEM((rows, heads * size), BF),
                pltpu.VMEM((rows, heads * size), BF),
                pltpu.VMEM((heads, rows), F32),
                pltpu.VMEM((KINDS, heads, size, size), F32),
                pltpu.VMEM((KINDS, heads, size, size), BF),
                stack,
                pltpu.VMEM((slots, KINDS, size, size), BF),
                pltpu.VMEM((slots, KINDS, size, size), BF),
                stack, stack, stack, stack,
                pltpu.VMEM((KINDS, size, size), F32),
                pltpu.VMEM((KINDS, size, size), F32),
                pltpu.VMEM((KINDS, size, size), F32),
                pltpu.VMEM((KINDS, size, size), BF),
                pltpu.VMEM((KINDS, size, size), BF),
                pltpu.VMEM((heads, rows, size), BF),
                pltpu.VMEM((slots, 2 * nh, rows // nh, size), BF),
                dma((5, 2)),
                dma((2,)),
                dma((slots,)), dma((slots, KINDS)),
                dma((slots,)), dma((pieces,)),
                dma((slots,)), dma((pieces,)),
                dma((2,)), dma((nh - 1,)),
                dma((slots,)), dma((nh - 1,)), dma((slots,)), dma((slots,)),
            ],
            compiler_params=pltpu.CompilerParams(
                collective_id=0,
                has_side_effects=True,
                vmem_limit_bytes=VMEM_BYTES - out_bytes - 16384,
            ),
        )(queries, key_rows, value_rows, step_rates, gate_fast, up_fast, down_fast)

    placed = (
        P(None, "tok", "head"),
        P("tok", "head"),
        P("tok", "head"),
        P("head", "tok"),
        P("head", None, None),
        P("head", None, None),
        P("head", None, None),
    )
    return jax.shard_map(
        local, mesh=mesh, in_specs=placed, out_specs=P(None, ("tok", "head"), None), check_vma=False
    )
```

time: 51.6 us -> 45.5 us (0.88)
  Pallas kernels: 50.3 us -> 44.2 us
    pallas_call x1, Pallas kernels: 50.3 us -> 44.2 us  [local(): pl.pallas_call(functools.partial(kernel, nh, nz), out_shape=pltpu.VMEM(ou...]
where the time goes in v2:
time: 45.5 us; the launch traced here: 45.3 us
  Pallas kernels  44.2 us (97%)
  local copies, waits for them, and re-layouts  1.06 us (2%)
    pallas_call x1, Pallas kernels, local(): pl.pallas_call(functools.partial(kernel, nh, nz), out_shape=pltpu.VMEM(ou...  44.2 us
    unnamed x1, local copies, waits for them, and re-layouts  1.06 us

profile of v2, /device:TPU:0, one launch (start us, length us, event | category | flops | bytes accessed | tf_op | source)
XLA Modules:
  0.0 45.3 jit_solution(2243978140298825285)
XLA Ops:
  0.0 44.2 %shard_map.73 = bf16[2,64,5120]{2,1,0:T(8,128)(2,1)S(1)} custom-call(bf16[2,256,1280]{2,1,0:T(8,128)(2,1)} %q_in.1, bf16[256,1280]{1,0:T(8,128)(2,1)} %k_in.1, bf16[256,1280]{1,0:T(8,128)(2,1)} %v_in.1, f32[5,256]{1,0:T(8,128)} %r_in.1, f32[5,256,256]{2,1,0:T(8,128)} %g_in.1, f32[5,256,256]{2,1,0:T(8,128)} %u_in.1, f32[5,256,256]{2,1,0:T(8,128)} %d_in.1), custom_call_target="tpu_custom_call" | custom-call | tf_op jit(solution)/shard_map/pallas_call | solution.py:534
  44.2 1.1 %copy.9 = bf16[2,64,5120]{2,1,0:T(8,128)(2,1)} copy(bf16[2,64,5120]{2,1,0:T(8,128)(2,1)S(1)} %shard_map.73) | data formatting | bytes 2621440

commit v3 on v2

--- a/solution.py
+++ b/solution.py
@@ -10,6 +10,7 @@
 NS_STEPS = 3
 KINDS = 3
 PIECES = 4
+PAIR = 2
 LAG = 5
 LAG_ALONE = 9
 VMEM_BYTES = 67043328
@@ -43,8 +44,8 @@
 
 def kernel(
     nh, nz, q_in, k_in, v_in, r_in, g_in, u_in, d_in, out,
-    qb, qn, kb, vb, rb, wf, wh, own, sent, got, pi, si, po, so, mg, xs, gm, pm, wn, ob, ox,
-    ld, qs, sw_s, sw_r, p_s, p_r, s_s, s_r, a_s, a_r, b_s, b_r, b_p, b_l,
+    qb, qn, kb, vb, rb, wf, wh, own, sent, got, pi, si, po, so, mg, xs, wn, ob, ox,
+    ld, qs, sw_s, sw_p, sw_r, p_s, p_r, s_s, s_r, a_s, a_r, b_s, b_r, b_p, b_l,
 ):
     heads, share, size = ob.shape[0], ob.shape[1] // nh, ob.shape[2]
     rows = nh * share
@@ -80,20 +81,22 @@
     def _():
         pl.semaphore_signal(barrier, inc=1, device_id=(hd, tok + 2), device_id_type=MESH)
 
-    pl.semaphore_signal(barrier, inc=1, device_id=partner, device_id_type=MESH)
-    for p in range(1, nh):
-        for c in range(2):
-            pl.semaphore_signal(
-                barrier, inc=1, device_id=(lax.rem(hd + p, nh), 2 * z + c), device_id_type=MESH
-            )
     inner = (z > 0).astype(jnp.int32) + (z < nz - 1).astype(jnp.int32)
+
+    def greet_plane():
+        pl.semaphore_signal(barrier, inc=1, device_id=partner, device_id_type=MESH)
+        for p in range(1, nh):
+            for c in range(2):
+                pl.semaphore_signal(
+                    barrier, inc=1, device_id=(lax.rem(hd + p, nh), 2 * z + c), device_id_type=MESH
+                )
 
     def load_head(stage, columns, some):
         pltpu.make_async_copy(k_in.at[:, columns], kb.at[:, columns], ld.at[stage, 0]).start()
-        for k, src in enumerate((g_in, u_in)):
+        for k, src in ((1, g_in), (2, u_in)):
             pltpu.make_async_copy(src.at[some], wf.at[k, some], ld.at[stage, 1]).start()
         pltpu.make_async_copy(v_in.at[:, columns], vb.at[:, columns], ld.at[stage, 0]).start()
-        pltpu.make_async_copy(d_in.at[some], wf.at[2, some], ld.at[stage, 1]).start()
+        pltpu.make_async_copy(d_in.at[some], wf.at[0, some], ld.at[stage, 1]).start()
 
     def wait_head(stage, count):
         both = q_in.at[:, :, pl.ds(0, count * size)]
@@ -101,9 +104,20 @@
         three = wf.at[:, pl.ds(0, count)]
         pltpu.make_async_copy(three, three, ld.at[stage, 1]).wait()
 
+    def opening():
+        h = theirs(0)
+        some = pl.ds(h, 1)
+        keys = pltpu.make_async_copy(k_in.at[:, cut(h)], kb.at[:, cut(h)], ld.at[0, 0])
+        values = pltpu.make_async_copy(v_in.at[:, cut(h)], vb.at[:, cut(h)], ld.at[0, 1])
+        gates = pltpu.make_async_copy(g_in.at[some], wf.at[1, some], ld.at[3, 1])
+        ups = pltpu.make_async_copy(u_in.at[some], wf.at[2, some], ld.at[3, 1])
+        downs = pltpu.make_async_copy(d_in.at[some], wf.at[0, some], ld.at[4, 1])
+        return keys, gates, ups, values, downs, load_rates
+
     load_rates = pltpu.make_async_copy(r_in, rb, ld.at[3, 0])
-    load_first = pltpu.make_async_copy(q_in.at[0], qb, ld.at[3, 1])
+    load_first = pltpu.make_async_copy(q_in.at[0], qb, ld.at[4, 0])
     load_next = pltpu.make_async_copy(q_in.at[1], qn.at[lane], ld.at[4, 0])
+    load_both = pltpu.make_async_copy(q_in, q_in, ld.at[4, 0])
     push_next = pltpu.make_async_remote_copy(
         q_in.at[1], qn.at[lane], qs.at[0], qs.at[1], device_id=partner, device_id_type=MESH
     )
@@ -111,10 +125,15 @@
     def place(t):
         return t // PIECES, pl.ds(pl.multiple_of(lax.rem(t, PIECES) * piece, piece), piece)
 
+    def place_right(t):
+        span = PAIR * piece
+        each = PIECES // PAIR
+        return t // each, pl.ds(pl.multiple_of(lax.rem(t, each) * span, span), span)
+
     def right(src, t):
-        m, part = place(t)
+        m, part = place_right(t)
         return pltpu.make_async_remote_copy(
-            src.at[m, part], pi.at[m, part], p_s.at[t // per], p_r.at[t],
+            src.at[m, part], pi.at[m, part], p_s.at[t // (per // PAIR)], p_r.at[t],
             device_id=(hd, tok + 2), device_id_type=MESH,
         )
 
@@ -127,7 +146,14 @@
 
     def swap(i, k):
         return pltpu.make_async_remote_copy(
-            sent.at[i, k], got.at[i, k], sw_s.at[i], sw_r.at[i, k],
+            sent.at[i, k], got.at[i, k], sw_s.at[i], sw_r.at[i],
+            device_id=partner, device_id_type=MESH,
+        )
+
+    def swap_piece(g):
+        part = pl.ds(g * piece, piece)
+        return pltpu.make_async_remote_copy(
+            sent.at[0, 0, part], got.at[0, 0, part], sw_s.at[0], sw_p.at[g],
             device_id=partner, device_id_type=MESH,
         )
 
@@ -167,47 +193,82 @@
             ox.at[i, lane * nh + hd], out.at[1, :, wide(mine(i))], b_l.at[i]
         )
 
-    def gradients(h):
+    def gradients(h, put, await_early=None, await_late=None):
+        if await_early is not None:
+            await_early()
         keys = kb[:, cut(h)]
-        gate = wf[0, h].astype(BF)
-        up = wf[1, h].astype(BF)
-        down = wf[2, h].astype(BF)
-        wh[0, h] = gate
-        wh[1, h] = up
-        wh[2, h] = down
+        gate = wf[1, h].astype(BF)
+        up = wf[2, h].astype(BF)
+        wh[1, h] = gate
+        wh[2, h] = up
         zg = mm(keys, gate)
         zu = mm(keys, up)
         sig = 1.0 / (1.0 + jnp.exp(-zg))
         silu = zg * sig
         hidden = (silu * zu).astype(BF)
+        if await_late is not None:
+            await_late()
+        down = wf[0, h].astype(BF)
+        wh[0, h] = down
         line = jnp.broadcast_to(rb[pl.ds(h, 1), :], (128, rows))
         column = jnp.transpose(line)
         column = jnp.concatenate([column] * (size // 128), axis=1)
         dout = (-(column * vb[:, cut(h)].astype(F32))).astype(BF)
+        put(0, mm_tn(hidden, dout))
         dh = mm_nt(dout, down)
         dzu = (dh * silu).astype(BF)
         dzg = (dh * zu * sig * (1.0 + zg * (1.0 - sig))).astype(BF)
-        return mm_tn(keys, dzg), mm_tn(keys, dzu), mm_tn(hidden, dout)
-
-    def gradients_theirs(i):
-        parts = gradients(theirs(i))
-        for k in range(KINDS):
-            sent[i, k] = parts[k].astype(BF)
+        put(1, mm_tn(keys, dzg))
+        put(2, mm_tn(keys, dzu))
+
+    def gradients_theirs(i, before=lambda k: None, waits=()):
+        def put(k, part):
+            sent[i, k] = part.astype(BF)
+            before(k)
+            if isinstance(i, int) and k == 0:
+                for g in range(PIECES):
+                    swap_piece(g).start()
+            else:
+                swap(i, k).start()
+
+        gradients(theirs(i), put, *waits)
 
     def gradients_mine(i):
-        parts = gradients(mine(i))
-        for k in range(KINDS):
-            mg[k] = parts[k]
+        def put(k, part):
+            mg[k] = part
+
+        gradients(mine(i), put)
+
+    def add_first():
+        for g in range(PIECES):
+            part = pl.ds(g * piece, piece)
+            swap_piece(g).wait_recv()
+            own[0, part] = (mg[0, part] + got[0, 0, part].astype(F32)).astype(BF)
+
+            @pl.when(last_end)
+            def _():
+                left(own, g).start()
+
+            if g % PAIR == PAIR - 1:
+
+                @pl.when(first_end)
+                def _():
+                    right(own, g // PAIR).start()
 
     def add_theirs(i):
-        for k in range(KINDS):
-            swap(i, k).wait_recv()
+        early = isinstance(i, int) and i == 0
+        if early:
+            add_first()
+        begin = 1 if early else 0
+        rest_of = got.at[i, pl.ds(begin, KINDS - begin)]
+        pltpu.make_async_copy(rest_of, rest_of, sw_r.at[i]).wait()
+        for k in range(begin, KINDS):
             own[KINDS * i + k] = (mg[k] + got[i, k].astype(F32)).astype(BF)
 
             @pl.when(first_end)
             def _():
-                for g in range(PIECES):
-                    right(own, per * i + k * PIECES + g).start()
+                for g in range(PIECES // PAIR):
+                    right(own, (KINDS * i + k) * (PIECES // PAIR) + g).start()
 
             @pl.when(last_end)
             def _():
@@ -226,12 +287,13 @@
         p = turn(t, z - 1)
         s = turn(t, nz - 2 - z)
 
-        @pl.when(middle & (p >= 0) & (p < total))
-        def _():
-            m, part = place(p)
-            right(po, p).wait_recv()
+        @pl.when(middle & (p >= 0) & (p < total) & (lax.rem(p, PAIR) == PAIR - 1))
+        def _():
+            n = p // PAIR
+            m, part = place_right(n)
+            right(po, n).wait_recv()
             po[m, part] = (pi[m, part].astype(F32) + own[m, part].astype(F32)).astype(BF)
-            right(po, p).start()
+            right(po, n).start()
 
         @pl.when(middle & (s >= 0) & (s < total))
         def _():
@@ -241,7 +303,7 @@
             left(so, s).start()
 
     def first(h):
-        ob[h] = fast_apply(qb[:, cut(h)], wh[0, h], wh[1, h], wh[2, h])
+        ob[h] = fast_apply(qb[:, cut(h)], wh[1, h], wh[2, h], wh[0, h])
         for p in order[:-1]:
             deal(h, p).start()
         keep(h).start()
@@ -258,8 +320,8 @@
 
             @pl.when(last_end)
             def _():
-                for g in range(PIECES):
-                    right(own, per * i + k * PIECES + g).wait_recv()
+                for g in range(PIECES // PAIR):
+                    right(own, (KINDS * i + k) * (PIECES // PAIR) + g).wait_recv()
                 xs[k] = own[m].astype(F32) + pi[m].astype(F32)
 
             @pl.when(middle)
@@ -275,21 +337,7 @@
         gather_some(i, range(KINDS - 1))
         gather_some(i, [KINDS - 1])
 
-    def gram_all():
-        for k in range(KINDS):
-            x = xs[k].astype(BF)
-            gm[k] = mm_nt(x, x)
-
-    def poly_all():
-        for k in range(KINDS):
-            half = gm[k].astype(BF)
-            pm[k] = (coef_second * gm[k] + coef_third * mm(half, half)).astype(BF)
-
-    def apply_all():
-        for k in range(KINDS):
-            xs[k] = coef_first * xs[k] + mm(pm[k], xs[k].astype(BF))
-
-    def sweep():
+    def sweep(i=None):
         x = [xs[k] for k in range(KINDS)]
         xb = [v.astype(BF) for v in x]
         gram = [mm_nt(v, v) for v in xb]
@@ -297,15 +345,16 @@
         square = [mm(v, v) for v in half]
         poly = [(coef_second * a + coef_third * b).astype(BF) for a, b in zip(gram, square)]
         for k in range(KINDS):
-            xs[k] = coef_first * x[k] + mm(poly[k], xb[k])
-
-    def update(i):
-        for k in range(KINDS):
-            wn[k] = (wf[k, mine(i)] - xs[k]).astype(BF)
+            y = coef_first * x[k] + mm(poly[k], xb[k])
+            if i is None:
+                xs[k] = y
+            else:
+                wn[k] = (wf[k, mine(i)] - y).astype(BF)
+
 
     def second(i):
         x = qn[:, :, cut(mine(i))].reshape(2 * rows, size)
-        ox[i] = fast_apply(x, wn[0], wn[1], wn[2]).reshape(2 * nh, share, size)
+        ox[i] = fast_apply(x, wn[1], wn[2], wn[0]).reshape(2 * nh, share, size)
         for p in order:
             for c in range(2):
                 if p > 0:
@@ -322,8 +371,6 @@
         @pl.when(theirs(i) < heads)
         def _():
             gradients_theirs(i)
-            for k in range(KINDS):
-                swap(i, k).start()
 
     def add_mine(i):
         @pl.when(mine(i) < heads)
@@ -341,22 +388,34 @@
         def _():
             first(h)
 
-    load_rates.start()
-    load_head(0, cut(theirs(0)), pl.ds(theirs(0), 1))
+    first_loads = opening()
+    for copy in first_loads:
+        copy.start()
+    greet_plane()
     load_head(1, cut(mine(0)), pl.ds(mine(0), 1))
-    load_rates.wait()
-    wait_head(0, 1)
-    if heads > 2:
-        rest = heads - 2
-        load_head(2, pl.ds(2 * size, rest * size), pl.ds(2, rest))
-    load_first.start()
-    load_next.start()
-    gradients_theirs(0)
+    rest = heads - 2
+
+    def early_waits():
+        first_loads[0].wait()
+        two = wf.at[pl.ds(1, 2), theirs(0)]
+        pltpu.make_async_copy(two, two, ld.at[3, 1]).wait()
+
+    def late_waits():
+        for copy in first_loads[3:]:
+            copy.wait()
+        if rest > 0:
+            load_head(2, pl.ds(2 * size, rest * size), pl.ds(2, rest))
+        load_first.start()
+        load_next.start()
+
+
+    def enter(k):
+        if k == 0:
+            pl.semaphore_wait(barrier, 1 + 2 * (nh - 1) + inner)
+
+    gradients_theirs(0, enter, (early_waits, late_waits))
     wait_head(1, 1)
     gradients_mine(0)
-    pl.semaphore_wait(barrier, 1 + 2 * (nh - 1) + inner)
-    for k in range(KINDS):
-        swap(0, k).start()
     add_theirs(0)
     if heads > 2:
         wait_head(2, rest)
@@ -377,11 +436,7 @@
     behind, offset = late // per, late % per
     defer = middle & (mine(slots - 1) < heads)
 
-    def finish(i):
-        update(i)
-        second(i)
-
-    load_first.wait()
+    load_both.wait()
 
     @pl.loop(0, slots + behind)
     def _(r):
@@ -399,7 +454,6 @@
         def begin():
             @pl.when(i == 0)
             def _():
-                load_next.wait()
                 push_next.wait_recv()
 
             gather(i)
@@ -410,7 +464,7 @@
         for n in range(firsts):
             work[2 * n + 3] = [lambda n=n: first_of(firsts * r + n)]
         tail = []
-        for n, item in enumerate([begin, None, sweep, sweep, None, sweep, lambda: finish(i)]):
+        for n, item in enumerate([begin, None, sweep, sweep, None, lambda: sweep(i), lambda: second(i)]):
             if item is None:
                 continue
             if start + n < per:
@@ -430,55 +484,24 @@
         for item in tail:
             item()
 
-    def last_wait(i):
-        if slots <= 2:
-
-            @pl.when(i == 0)
-            def _():
-                load_next.wait()
-                push_next.wait_recv()
-
-    begun = per * (slots + behind)
-    ended = per * slots + LAG_ALONE * hops
-    held = max(slots - 2, 0)
-    small = [lambda k=k: gather_some(held, [k]) for k in range(KINDS)]
-    small += [gram_all, poly_all, apply_all] * NS_STEPS
-    if nz == 4 and slots > 1:
-        for t in range(begun, ended):
-            pass_on(t)
-
-            @pl.when(defer)
-            def _():
-                if t == begun:
-                    last_wait(held)
-                n = t - begun
-                for run in small[n * len(small) // (ended - begun) : (n + 1) * len(small) // (ended - begun)]:
-                    run()
-    else:
-
-        @pl.loop(begun, ended)
-        def _(t):
-            pass_on(t)
-
-        @pl.when(defer)
-        def _():
-            last_wait(held)
-            for run in small:
-                run()
-
-    @pl.when(defer)
-    def _():
-        if slots > 1:
-            finish(held)
-
-    @pl.when(mine(slots - 1) < heads)
-    def _():
-        if slots == 1:
-            last_wait(0)
-        gather(slots - 1)
-        for s in range(NS_STEPS):
-            sweep()
-        finish(slots - 1)
+    @pl.loop(per * (slots + behind), per * slots + LAG_ALONE * hops)
+    def _(t):
+        pass_on(t)
+
+    @pl.loop(jnp.where(defer, max(slots - 2, 0), slots - 1), slots)
+    def _(i):
+        @pl.when(mine(i) < heads)
+        def _():
+            if slots <= 2:
+
+                @pl.when(i == 0)
+                def _():
+                        push_next.wait_recv()
+
+            gather(i)
+            for s in range(NS_STEPS):
+                sweep(i if s == NS_STEPS - 1 else None)
+            second(i)
 
     push_next.wait_send()
 
@@ -550,15 +573,13 @@
                 stack, stack, stack, stack,
                 pltpu.VMEM((KINDS, size, size), F32),
                 pltpu.VMEM((KINDS, size, size), F32),
-                pltpu.VMEM((KINDS, size, size), F32),
-                pltpu.VMEM((KINDS, size, size), BF),
                 pltpu.VMEM((KINDS, size, size), BF),
                 pltpu.VMEM((heads, rows, size), BF),
                 pltpu.VMEM((slots, 2 * nh, rows // nh, size), BF),
                 dma((5, 2)),
                 dma((2,)),
-                dma((slots,)), dma((slots, KINDS)),
-                dma((slots,)), dma((pieces,)),
+                dma((slots,)), dma((PIECES,)), dma((slots,)),
+                dma((slots,)), dma((pieces // PAIR,)),
                 dma((slots,)), dma((pieces,)),
                 dma((2,)), dma((nh - 1,)),
                 dma((slots,)), dma((nh - 1,)), dma((slots,)), dma((slots,)),

time: 45.5 us -> 44.3 us (0.974)
  Pallas kernels: 44.2 us -> 43.1 us
    pallas_call x1, Pallas kernels: 44.2 us -> 43.1 us  [local(): pl.pallas_call(functools.partial(kernel, nh, nz), out_shape=pltpu.VMEM(ou...]
where the time goes in v3:
time: 44.3 us; the launch traced here: 44.2 us
  Pallas kernels  43.1 us (97%)
  local copies, waits for them, and re-layouts  1.06 us (2%)
    pallas_call x1, Pallas kernels, local(): pl.pallas_call(functools.partial(kernel, nh, nz), out_shape=pltpu.VMEM(ou...  43.1 us
    unnamed x1, local copies, waits for them, and re-layouts  1.06 us

profile of v3, /device:TPU:0, one launch (start us, length us, event | category | flops | bytes accessed | tf_op | source)
XLA Modules:
  0.0 44.2 jit_solution(14194920171011070752)
XLA Ops:
  0.0 43.1 %shard_map.73 = bf16[2,64,5120]{2,1,0:T(8,128)(2,1)S(1)} custom-call(bf16[2,256,1280]{2,1,0:T(8,128)(2,1)} %q_in.1, bf16[256,1280]{1,0:T(8,128)(2,1)} %k_in.1, bf16[256,1280]{1,0:T(8,128)(2,1)} %v_in.1, f32[5,256]{1,0:T(8,128)} %r_in.1, f32[5,256,256]{2,1,0:T(8,128)} %g_in.1, f32[5,256,256]{2,1,0:T(8,128)} %u_in.1, f32[5,256,256]{2,1,0:T(8,128)} %d_in.1), custom_call_target="tpu_custom_call" | custom-call | tf_op jit(solution)/shard_map/pallas_call | solution.py:557
  43.1 1.1 %copy.9 = bf16[2,64,5120]{2,1,0:T(8,128)(2,1)} copy(bf16[2,64,5120]{2,1,0:T(8,128)(2,1)S(1)} %shard_map.73) | data formatting | bytes 2621440

commit v4 on v2

v4 whole, which is shorter than its diff:
```python
import functools

import jax
import jax.numpy as jnp
from jax import lax
from jax.experimental import pallas as pl
from jax.experimental.pallas import tpu as pltpu
from jax.sharding import PartitionSpec as P

NS_STEPS = 3
KINDS = 3
PIECES = 4
PAIR = 2
LAG = 5
LAG_ALONE = 9
VMEM_BYTES = 67043328

coef_first = 3.4445
coef_second = -4.775
coef_third = 2.0315

MESH = pl.DeviceIdType.MESH
BF = jnp.bfloat16
F32 = jnp.float32


def mm(a, b):
    return jnp.dot(a, b, preferred_element_type=F32)


def mm_tn(a, b):
    return lax.dot_general(a, b, (((0,), (0,)), ((), ())), preferred_element_type=F32)


def mm_nt(a, b):
    return lax.dot_general(a, b, (((1,), (1,)), ((), ())), preferred_element_type=F32)


def fast_apply(x, gate, up, down):
    pre = mm(x, gate)
    hidden = (pre / (1.0 + jnp.exp(-pre)) * mm(x, up)).astype(BF)
    return mm(hidden, down).astype(BF)


def kernel(
    nh, nz, q_in, k_in, v_in, r_in, g_in, u_in, d_in, out,
    qb, qn, kb, vb, rb, wf, wh, own, sent, got, pi, si, po, so, mg, xs, wn, ob, ox,
    a_s, a_r, b_s, b_r, b_p, b_l,
):
    heads, share, size = ob.shape[0], ob.shape[1] // nh, ob.shape[2]
    rows = nh * share
    slots = sent.shape[0]
    piece = size // PIECES
    per = KINDS * PIECES
    hd = lax.axis_index("head")
    tok = lax.axis_index("tok")
    lane = lax.rem(tok, 2)
    z = tok // 2
    partner = (hd, z * 2 + 1 - lane)
    total = per * ((heads + 1 - lane) // 2)
    first_end = z == 0
    last_end = z == nz - 1
    middle = jnp.logical_not(first_end) & jnp.logical_not(last_end)

    def cut(h):
        return pl.ds(h * size if isinstance(h, int) else pl.multiple_of(h * size, size), size)

    def mine(i):
        return 2 * i + lane

    def theirs(i):
        return 2 * i + 1 - lane

    def main(ld, qs, sw_s, sw_p, sw_r, p_s, p_r, s_s, s_r):
        barrier = pltpu.get_barrier_semaphore()

        inner = (z > 0).astype(jnp.int32) + (z < nz - 1).astype(jnp.int32)

        def greet_plane():
            pl.semaphore_signal(barrier, inc=1, device_id=partner, device_id_type=MESH)
            for p in range(1, nh):
                for c in range(2):
                    pl.semaphore_signal(
                        barrier, inc=1, device_id=(lax.rem(hd + p, nh), 2 * z + c), device_id_type=MESH
                    )

        def load_head(stage, columns, some):
            pltpu.make_async_copy(k_in.at[:, columns], kb.at[:, columns], ld.at[stage, 0]).start()
            for k, src in ((1, g_in), (2, u_in)):
                pltpu.make_async_copy(src.at[some], wf.at[k, some], ld.at[stage, 1]).start()
            pltpu.make_async_copy(v_in.at[:, columns], vb.at[:, columns], ld.at[stage, 0]).start()
            pltpu.make_async_copy(d_in.at[some], wf.at[0, some], ld.at[stage, 1]).start()

        def wait_head(stage, count):
            both = q_in.at[:, :, pl.ds(0, count * size)]
            pltpu.make_async_copy(both, both, ld.at[stage, 0]).wait()
            three = wf.at[:, pl.ds(0, count)]
            pltpu.make_async_copy(three, three, ld.at[stage, 1]).wait()

        def opening():
            h = theirs(0)
            some = pl.ds(h, 1)
            keys = pltpu.make_async_copy(k_in.at[:, cut(h)], kb.at[:, cut(h)], ld.at[0, 0])
            values = pltpu.make_async_copy(v_in.at[:, cut(h)], vb.at[:, cut(h)], ld.at[0, 1])
            gates = pltpu.make_async_copy(g_in.at[some], wf.at[1, some], ld.at[3, 1])
            ups = pltpu.make_async_copy(u_in.at[some], wf.at[2, some], ld.at[3, 1])
            downs = pltpu.make_async_copy(d_in.at[some], wf.at[0, some], ld.at[4, 1])
            return keys, gates, ups, values, downs, load_rates

        load_rates = pltpu.make_async_copy(r_in, rb, ld.at[3, 0])
        load_first = pltpu.make_async_copy(q_in.at[0], qb, ld.at[4, 0])
        load_next = pltpu.make_async_copy(q_in.at[1], qn.at[lane], ld.at[4, 0])
        load_both = pltpu.make_async_copy(q_in, q_in, ld.at[4, 0])
        push_next = pltpu.make_async_remote_copy(
            q_in.at[1], qn.at[lane], qs.at[0], qs.at[1], device_id=partner, device_id_type=MESH
        )

        def place(t):
            return t // PIECES, pl.ds(pl.multiple_of(lax.rem(t, PIECES) * piece, piece), piece)

        def place_right(t):
            span = PAIR * piece
            each = PIECES // PAIR
            return t // each, pl.ds(pl.multiple_of(lax.rem(t, each) * span, span), span)

        def right(src, t):
            m, part = place_right(t)
            return pltpu.make_async_remote_copy(
                src.at[m, part], pi.at[m, part], p_s.at[t // (per // PAIR)], p_r.at[t],
                device_id=(hd, tok + 2), device_id_type=MESH,
            )

        def left(src, t):
            m, part = place(t)
            return pltpu.make_async_remote_copy(
                src.at[m, part], si.at[m, part], s_s.at[t // per], s_r.at[t],
                device_id=(hd, tok - 2), device_id_type=MESH,
            )

        def swap(i, k):
            return pltpu.make_async_remote_copy(
                sent.at[i, k], got.at[i, k], sw_s.at[i], sw_r.at[i],
                device_id=partner, device_id_type=MESH,
            )

        def swap_piece(g):
            part = pl.ds(g * piece, piece)
            return pltpu.make_async_remote_copy(
                sent.at[0, 0, part], got.at[0, 0, part], sw_s.at[0], sw_p.at[g],
                device_id=partner, device_id_type=MESH,
            )

        def wide(h):
            return pl.ds(pl.multiple_of((hd * heads + h) * size, size), size)

        def band(peer):
            return pl.ds(pl.multiple_of(peer * share, share), share)

        order = (3, 1, 2, 0) if nh == 4 else tuple(range(nh - 1, -1, -1))

        def other(p):
            if nh != 4 or p == 0:
                return lax.rem(hd + p, nh)
            return (hd + 1 - 2 * lax.rem(hd, 2), lax.rem(hd + 2, 4), 3 - hd)[p - 1]

        def deal(h, p):
            peer = other(p)
            return pltpu.make_async_remote_copy(
                ob.at[h, band(peer)], out.at[0, :, wide(h)], a_s.at[0], a_r.at[p - 1],
                device_id=(peer, tok), device_id_type=MESH,
            )

        def keep(h):
            return pltpu.make_async_copy(ob.at[h, band(hd)], out.at[0, :, wide(h)], a_s.at[1])

        def deal_next(i, c, p):
            peer = other(p)
            return pltpu.make_async_remote_copy(
                ox.at[i, c * nh + peer], out.at[1, :, wide(mine(i))],
                b_s.at[i], b_p.at[i] if p == 0 else b_r.at[p - 1],
                device_id=(peer, 2 * z + c), device_id_type=MESH,
            )

        def keep_next(i):
            return pltpu.make_async_copy(
                ox.at[i, lane * nh + hd], out.at[1, :, wide(mine(i))], b_l.at[i]
            )

        def gradients(h, put, await_early=None, await_late=None):
            if await_early is not None:
                await_early()
            keys = kb[:, cut(h)]
            gate = wf[1, h].astype(BF)
            up = wf[2, h].astype(BF)
            wh[1, h] = gate
            wh[2, h] = up
            zg = mm(keys, gate)
            zu = mm(keys, up)
            sig = 1.0 / (1.0 + jnp.exp(-zg))
            silu = zg * sig
            hidden = (silu * zu).astype(BF)
            if await_late is not None:
                await_late()
            down = wf[0, h].astype(BF)
            wh[0, h] = down
            line = jnp.broadcast_to(rb[pl.ds(h, 1), :], (128, rows))
            column = jnp.transpose(line)
            column = jnp.concatenate([column] * (size // 128), axis=1)
            dout = (-(column * vb[:, cut(h)].astype(F32))).astype(BF)
            put(0, mm_tn(hidden, dout))
            dh = mm_nt(dout, down)
            dzu = (dh * silu).astype(BF)
            dzg = (dh * zu * sig * (1.0 + zg * (1.0 - sig))).astype(BF)
            put(1, mm_tn(keys, dzg))
            put(2, mm_tn(keys, dzu))

        def gradients_theirs(i, before=lambda k: None, waits=()):
            def put(k, part):
                sent[i, k] = part.astype(BF)
                before(k)
                if isinstance(i, int) and k == 0:
                    for g in range(PIECES):
                        swap_piece(g).start()
                else:
                    swap(i, k).start()

            gradients(theirs(i), put, *waits)

        def gradients_mine(i):
            def put(k, part):
                mg[k] = part

            gradients(mine(i), put)

        def add_first():
            for g in range(PIECES):
                part = pl.ds(g * piece, piece)
                swap_piece(g).wait_recv()
                own[0, part] = (mg[0, part] + got[0, 0, part].astype(F32)).astype(BF)

                @pl.when(last_end)
                def _():
                    left(own, g).start()

                if g % PAIR == PAIR - 1:

                    @pl.when(first_end)
                    def _():
                        right(own, g // PAIR).start()

        def add_theirs(i):
            early = isinstance(i, int) and i == 0
            if early:
                add_first()
            begin = 1 if early else 0
            rest_of = got.at[i, pl.ds(begin, KINDS - begin)]
            pltpu.make_async_copy(rest_of, rest_of, sw_r.at[i]).wait()
            for k in range(begin, KINDS):
                own[KINDS * i + k] = (mg[k] + got[i, k].astype(F32)).astype(BF)

                @pl.when(first_end)
                def _():
                    for g in range(PIECES // PAIR):
                        right(own, (KINDS * i + k) * (PIECES // PAIR) + g).start()

                @pl.when(last_end)
                def _():
                    for g in range(PIECES):
                        left(own, per * i + k * PIECES + g).start()

        turn_at = per * (slots - 1)
        alone = (mine(slots - 1) < heads) & (theirs(slots - 1) >= heads)

        def turn(t, far):
            fast = (LAG_ALONE - LAG) * far
            held = jnp.where(t < turn_at + fast, -1, t - LAG_ALONE * far)
            return jnp.where(alone & (t >= turn_at), held, t - LAG * far)

        def pass_on(t):
            p = turn(t, z - 1)
            s = turn(t, nz - 2 - z)

            @pl.when(middle & (p >= 0) & (p < total) & (lax.rem(p, PAIR) == PAIR - 1))
            def _():
                n = p // PAIR
                m, part = place_right(n)
                right(po, n).wait_recv()
                po[m, part] = (pi[m, part].astype(F32) + own[m, part].astype(F32)).astype(BF)
                right(po, n).start()

            @pl.when(middle & (s >= 0) & (s < total))
            def _():
                m, part = place(s)
                left(so, s).wait_recv()
                so[m, part] = (si[m, part].astype(F32) + own[m, part].astype(F32)).astype(BF)
                left(so, s).start()

        def first(h):
            ob[h] = fast_apply(qb[:, cut(h)], wh[1, h], wh[2, h], wh[0, h])
            for p in order[:-1]:
                deal(h, p).start()
            keep(h).start()

        def gather_some(i, kinds):
            for k in kinds:
                m = KINDS * i + k

                @pl.when(first_end)
                def _():
                    for g in range(PIECES):
                        left(own, per * i + k * PIECES + g).wait_recv()
                    xs[k] = own[m].astype(F32) + si[m].astype(F32)

                @pl.when(last_end)
                def _():
                    for g in range(PIECES // PAIR):
                        right(own, (KINDS * i + k) * (PIECES // PAIR) + g).wait_recv()
                    xs[k] = own[m].astype(F32) + pi[m].astype(F32)

                @pl.when(middle)
                def _():
                    xs[k] = own[m].astype(F32) + pi[m].astype(F32) + si[m].astype(F32)

            grads = [xs[k] for k in kinds]
            scales = [1.0 / (jnp.sqrt(jnp.sum(v * v)) + 1e-07) for v in grads]
            for k, v, scale in zip(kinds, grads, scales):
                xs[k] = v * scale

        def gather(i):
            gather_some(i, range(KINDS - 1))
            gather_some(i, [KINDS - 1])

        def sweep(i=None):
            x = [xs[k] for k in range(KINDS)]
            xb = [v.astype(BF) for v in x]
            gram = [mm_nt(v, v) for v in xb]
            half = [v.astype(BF) for v in gram]
            square = [mm(v, v) for v in half]
            poly = [(coef_second * a + coef_third * b).astype(BF) for a, b in zip(gram, square)]
            for k in range(KINDS):
                y = coef_first * x[k] + mm(poly[k], xb[k])
                if i is None:
                    xs[k] = y
                else:
                    wn[k] = (wf[k, mine(i)] - y).astype(BF)


        def second(i):
            x = qn[:, :, cut(mine(i))].reshape(2 * rows, size)
            ox[i] = fast_apply(x, wn[1], wn[2], wn[0]).reshape(2 * nh, share, size)
            for p in order:
                for c in range(2):
                    if p > 0:
                        deal_next(i, c, p).start()
                    else:

                        @pl.when(lane != c)
                        def _():
                            deal_next(i, c, p).start()

            keep_next(i).start()

        def ready_theirs(i):
            @pl.when(theirs(i) < heads)
            def _():
                gradients_theirs(i)

        def add_mine(i):
            @pl.when(mine(i) < heads)
            def _():
                add_theirs(i)

        def ready_mine(i):
            @pl.when((i < slots) & (mine(i) < heads))
            def _():
                gradients_mine(i)
                add_theirs(i)

        def first_of(h):
            @pl.when(h < heads)
            def _():
                first(h)

        first_loads = opening()
        for copy in first_loads:
            copy.start()

        @pl.when(z > 0)
        def _():
            pl.semaphore_signal(barrier, inc=1, device_id=(hd, tok - 2), device_id_type=MESH)

        @pl.when(z < nz - 1)
        def _():
            pl.semaphore_signal(barrier, inc=1, device_id=(hd, tok + 2), device_id_type=MESH)

        greet_plane()
        load_head(1, cut(mine(0)), pl.ds(mine(0), 1))
        rest = heads - 2

        def early_waits():
            first_loads[0].wait()
            two = wf.at[pl.ds(1, 2), theirs(0)]
            pltpu.make_async_copy(two, two, ld.at[3, 1]).wait()

        def late_waits():
            for copy in first_loads[3:]:
                copy.wait()
            if rest > 0:
                load_head(2, pl.ds(2 * size, rest * size), pl.ds(2, rest))
            load_first.start()
            load_next.start()


        def enter(k):
            if k == 0:
                pl.semaphore_wait(barrier, 1 + 2 * (nh - 1) + inner)

        gradients_theirs(0, enter, (early_waits, late_waits))
        wait_head(1, 1)
        gradients_mine(0)
        add_theirs(0)
        if heads > 2:
            wait_head(2, rest)

            @pl.loop(1, slots)
            def _(i):
                ready_theirs(i)

        push_next.start()
        if slots > 1:

            @pl.when(mine(1) < heads)
            def _():
                gradients_mine(1)

        hops = max(nz - 3, 0)
        late = LAG * hops if turn_at - LAG * hops >= per * (slots - 2) else LAG_ALONE * hops
        behind, offset = late // per, late % per
        defer = middle & (mine(slots - 1) < heads)

        load_both.wait()

        @pl.loop(0, slots + behind)
        def _(r):
            base = per * r
            i = r - 1 - behind

            def done(work):
                def run():
                    @pl.when((i >= 0) & jnp.logical_not(defer & (i == slots - 2)))
                    def _():
                        work()

                return run

            def begin():
                @pl.when(i == 0)
                def _():
                    push_next.wait_recv()

                gather(i)

            start = offset
            work = {1: [lambda: ready_mine(r + 2)]}
            firsts = (heads + 1) // 2
            for n in range(firsts):
                work[2 * n + 3] = [lambda n=n: first_of(firsts * r + n)]
            tail = []
            for n, item in enumerate([begin, None, sweep, sweep, None, lambda: sweep(i), lambda: second(i)]):
                if item is None:
                    continue
                if start + n < per:
                    work.setdefault(start + n, []).append(done(item))
                else:
                    tail.append(done(item))
            for t in range(per):
                pass_on(base + t)
                if t == 0 and slots > 1:

                    @pl.when(r == 0)
                    def _():
                        add_mine(1)

                for item in work.get(t, []):
                    item()
            for item in tail:
                item()

        @pl.loop(per * (slots + behind), per * slots + LAG_ALONE * hops)
        def _(t):
            pass_on(t)

        @pl.loop(jnp.where(defer, max(slots - 2, 0), slots - 1), slots)
        def _(i):
            @pl.when(mine(i) < heads)
            def _():
                if slots <= 2:

                    @pl.when(i == 0)
                    def _():
                            push_next.wait_recv()

                gather(i)
                for s in range(NS_STEPS):
                    sweep(i if s == NS_STEPS - 1 else None)
                second(i)

        push_next.wait_send()

        @pl.loop(0, slots)
        def _(i):
            @pl.when(theirs(i) < heads)
            def _():
                pltpu.make_async_copy(sent.at[i], sent.at[i], sw_s.at[i]).wait()

            @pl.when(mine(i) < heads)
            def _():
                slot = own.at[pl.ds(KINDS * i, KINDS)]

                @pl.when(z < nz - 1)
                def _():
                    pltpu.make_async_copy(slot, slot, p_s.at[i]).wait()

                @pl.when(z > 0)
                def _():
                    pltpu.make_async_copy(slot, slot, s_s.at[i]).wait()

    dma = pltpu.SemaphoreType.DMA
    pieces = KINDS * slots * PIECES
    pl.run_scoped(
        main,
        dma((5, 2)), dma((2,)),
        dma((slots,)), dma((PIECES,)), dma((slots,)),
        dma((slots,)), dma((pieces // PAIR,)),
        dma((slots,)), dma((pieces,)),
    )

    @pl.loop(0, slots)
    def _(i):
        part = ox.at[i, 0]

        @pl.when(theirs(i) < heads)
        def _():
            pltpu.make_async_copy(part, part, b_p.at[i]).wait()

        @pl.when(mine(i) < heads)
        def _():
            most = ox.at[i, pl.ds(0, 2 * nh - 1)]
            pltpu.make_async_copy(most, most, b_s.at[i]).wait()
            pltpu.make_async_copy(part, part, b_l.at[i]).wait()

    part = ob.at[:, pl.ds(0, (nh - 1) * share)]
    pltpu.make_async_copy(part, part, a_s.at[0]).wait()
    part = ob.at[:, pl.ds(0, share)]
    pltpu.make_async_copy(part, part, a_s.at[1]).wait()
    for p in range(1, nh):
        part = out.at[0, :, pl.ds(0, heads * size)]
        pltpu.make_async_copy(part, part, a_r.at[p - 1]).wait()
        part = out.at[1, :, pl.ds(0, heads * size)]
        pltpu.make_async_copy(part, part, b_r.at[p - 1]).wait()


def solution(mesh):
    nh = mesh.shape["head"]
    nz = mesh.shape["tok"] // 2

    def local(queries, key_rows, value_rows, step_rates, gate_fast, up_fast, down_fast):
        heads, size, _ = gate_fast.shape
        rows = key_rows.shape[0]
        slots = (heads + 1) // 2
        matrices = KINDS * slots
        out_shape = (2, rows // nh, nh * heads * size)
        out_bytes = 2 * out_shape[0] * out_shape[1] * out_shape[2]
        anywhere = pl.BlockSpec(memory_space=pl.ANY)
        dma = pltpu.SemaphoreType.DMA
        stack = pltpu.VMEM((matrices, size, size), BF)
        return pl.pallas_call(
            functools.partial(kernel, nh, nz),
            out_shape=pltpu.VMEM(out_shape, BF),
            in_specs=[anywhere] * 7,
            out_specs=pl.BlockSpec(memory_space=pltpu.VMEM),
            scratch_shapes=[
                pltpu.VMEM((rows, heads * size), BF),
                pltpu.VMEM((2, rows, heads * size), BF),
                pltpu.VMEM((rows, heads * size), BF),
                pltpu.VMEM((rows, heads * size), BF),
                pltpu.VMEM((heads, rows), F32),
                pltpu.VMEM((KINDS, heads, size, size), F32),
                pltpu.VMEM((KINDS, heads, size, size), BF),
                stack,
                pltpu.VMEM((slots, KINDS, size, size), BF),
                pltpu.VMEM((slots, KINDS, size, size), BF),
                stack, stack, stack, stack,
                pltpu.VMEM((KINDS, size, size), F32),
                pltpu.VMEM((KINDS, size, size), F32),
                pltpu.VMEM((KINDS, size, size), BF),
                pltpu.VMEM((heads, rows, size), BF),
                pltpu.VMEM((slots, 2 * nh, rows // nh, size), BF),
                dma((2,)), dma((nh - 1,)),
                dma((slots,)), dma((nh - 1,)), dma((slots,)), dma((slots,)),
            ],
            compiler_params=pltpu.CompilerParams(
                collective_id=0,
                has_side_effects=True,
                vmem_limit_bytes=VMEM_BYTES - out_bytes - 16384,
            ),
        )(queries, key_rows, value_rows, step_rates, gate_fast, up_fast, down_fast)

    placed = (
        P(None, "tok", "head"),
        P("tok", "head"),
        P("tok", "head"),
        P("head", "tok"),
        P("head", None, None),
        P("head", None, None),
        P("head", None, None),
    )
    return jax.shard_map(
        local, mesh=mesh, in_specs=placed, out_specs=P(None, ("tok", "head"), None), check_vma=False
    )
```

time: 45.5 us -> 43.6 us (0.958)
  Pallas kernels: 44.2 us -> 42.4 us
    pallas_call x1, Pallas kernels: 44.2 us -> 42.4 us  [local(): pl.pallas_call(functools.partial(kernel, nh, nz), out_shape=pltpu.VMEM(ou...]
where the time goes in v4:
time: 43.6 us; the launch traced here: 43.5 us
  Pallas kernels  42.4 us (97%)
  local copies, waits for them, and re-layouts  1.06 us (2%)
    pallas_call x1, Pallas kernels, local(): pl.pallas_call(functools.partial(kernel, nh, nz), out_shape=pltpu.VMEM(ou...  42.4 us
    unnamed x1, local copies, waits for them, and re-layouts  1.06 us

profile of v4, /device:TPU:0, one launch (start us, length us, event | category | flops | bytes accessed | tf_op | source)
XLA Modules:
  0.0 43.5 jit_solution(6234783827682344482)
XLA Ops:
  0.0 42.4 %shard_map.73 = bf16[2,64,5120]{2,1,0:T(8,128)(2,1)S(1)} custom-call(bf16[2,256,1280]{2,1,0:T(8,128)(2,1)} %q_in.1, bf16[256,1280]{1,0:T(8,128)(2,1)} %k_in.1, bf16[256,1280]{1,0:T(8,128)(2,1)} %v_in.1, f32[5,256]{1,0:T(8,128)} %r_in.1, f32[5,256,256]{2,1,0:T(8,128)} %g_in.1, f32[5,256,256]{2,1,0:T(8,128)} %u_in.1, f32[5,256,256]{2,1,0:T(8,128)} %d_in.1), custom_call_target="tpu_custom_call" | custom-call | tf_op jit(solution)/shard_map/pallas_call | solution.py:577
  42.4 1.1 %copy.9 = bf16[2,64,5120]{2,1,0:T(8,128)(2,1)} copy(bf16[2,64,5120]{2,1,0:T(8,128)(2,1)S(1)} %shard_map.73) | data formatting | bytes 2621440

commit v5 on v4

--- a/solution.py
+++ b/solution.py
@@ -9,10 +9,10 @@
 
 NS_STEPS = 3
 KINDS = 3
-PIECES = 4
+PIECES = 8
 PAIR = 2
-LAG = 5
-LAG_ALONE = 9
+LAG = 10
+LAG_ALONE = 18
 VMEM_BYTES = 67043328
 
 coef_first = 3.4445
@@ -45,7 +45,6 @@
 def kernel(
     nh, nz, q_in, k_in, v_in, r_in, g_in, u_in, d_in, out,
     qb, qn, kb, vb, rb, wf, wh, own, sent, got, pi, si, po, so, mg, xs, wn, ob, ox,
-    a_s, a_r, b_s, b_r, b_p, b_l,
 ):
     heads, share, size = ob.shape[0], ob.shape[1] // nh, ob.shape[2]
     rows = nh * share
@@ -71,7 +70,7 @@
     def theirs(i):
         return 2 * i + 1 - lane
 
-    def main(ld, qs, sw_s, sw_p, sw_r, p_s, p_r, s_s, s_r):
+    def main(ld, qs, sw_s, sw_p, sw_r, p_s, p_r, s_s, s_r, a_s, a_r, b_s, b_r, b_p, b_l):
         barrier = pltpu.get_barrier_semaphore()
 
         inner = (z > 0).astype(jnp.int32) + (z < nz - 1).astype(jnp.int32)
@@ -461,16 +460,17 @@
                 gather(i)
 
             start = offset
-            work = {1: [lambda: ready_mine(r + 2)]}
+            stride = max(PIECES // 4, 1)
+            work = {stride: [lambda: ready_mine(r + 2)]}
             firsts = (heads + 1) // 2
             for n in range(firsts):
-                work[2 * n + 3] = [lambda n=n: first_of(firsts * r + n)]
+                work[stride * (2 * n + 3)] = [lambda n=n: first_of(firsts * r + n)]
             tail = []
             for n, item in enumerate([begin, None, sweep, sweep, None, lambda: sweep(i), lambda: second(i)]):
                 if item is None:
                     continue
-                if start + n < per:
-                    work.setdefault(start + n, []).append(done(item))
+                if start + stride * n < per:
+                    work.setdefault(start + stride * n, []).append(done(item))
                 else:
                     tail.append(done(item))
             for t in range(per):
@@ -524,6 +524,30 @@
                 @pl.when(z > 0)
                 def _():
                     pltpu.make_async_copy(slot, slot, s_s.at[i]).wait()
+
+        @pl.loop(0, slots)
+        def _(i):
+            part = ox.at[i, 0]
+
+            @pl.when(theirs(i) < heads)
+            def _():
+                pltpu.make_async_copy(part, part, b_p.at[i]).wait()
+
+            @pl.when(mine(i) < heads)
+            def _():
+                most = ox.at[i, pl.ds(0, 2 * nh - 1)]
+                pltpu.make_async_copy(most, most, b_s.at[i]).wait()
+                pltpu.make_async_copy(part, part, b_l.at[i]).wait()
+
+        part = ob.at[:, pl.ds(0, (nh - 1) * share)]
+        pltpu.make_async_copy(part, part, a_s.at[0]).wait()
+        part = ob.at[:, pl.ds(0, share)]
+        pltpu.make_async_copy(part, part, a_s.at[1]).wait()
+        for p in range(1, nh):
+            part = out.at[0, :, pl.ds(0, heads * size)]
+            pltpu.make_async_copy(part, part, a_r.at[p - 1]).wait()
+            part = out.at[1, :, pl.ds(0, heads * size)]
+            pltpu.make_async_copy(part, part, b_r.at[p - 1]).wait()
 
     dma = pltpu.SemaphoreType.DMA
     pieces = KINDS * slots * PIECES
@@ -533,31 +557,9 @@
         dma((slots,)), dma((PIECES,)), dma((slots,)),
         dma((slots,)), dma((pieces // PAIR,)),
         dma((slots,)), dma((pieces,)),
+        dma((2,)), dma((nh - 1,)),
+        dma((slots,)), dma((nh - 1,)), dma((slots,)), dma((slots,)),
     )
-
-    @pl.loop(0, slots)
-    def _(i):
-        part = ox.at[i, 0]
-
-        @pl.when(theirs(i) < heads)
-        def _():
-            pltpu.make_async_copy(part, part, b_p.at[i]).wait()
-
-        @pl.when(mine(i) < heads)
-        def _():
-            most = ox.at[i, pl.ds(0, 2 * nh - 1)]
-            pltpu.make_async_copy(most, most, b_s.at[i]).wait()
-            pltpu.make_async_copy(part, part, b_l.at[i]).wait()
-
-    part = ob.at[:, pl.ds(0, (nh - 1) * share)]
-    pltpu.make_async_copy(part, part, a_s.at[0]).wait()
-    part = ob.at[:, pl.ds(0, share)]
-    pltpu.make_async_copy(part, part, a_s.at[1]).wait()
-    for p in range(1, nh):
-        part = out.at[0, :, pl.ds(0, heads * size)]
-        pltpu.make_async_copy(part, part, a_r.at[p - 1]).wait()
-        part = out.at[1, :, pl.ds(0, heads * size)]
-        pltpu.make_async_copy(part, part, b_r.at[p - 1]).wait()
 
 
 def solution(mesh):
@@ -572,7 +574,6 @@
         out_shape = (2, rows // nh, nh * heads * size)
         out_bytes = 2 * out_shape[0] * out_shape[1] * out_shape[2]
         anywhere = pl.BlockSpec(memory_space=pl.ANY)
-        dma = pltpu.SemaphoreType.DMA
         stack = pltpu.VMEM((matrices, size, size), BF)
         return pl.pallas_call(
             functools.partial(kernel, nh, nz),
@@ -596,8 +597,6 @@
                 pltpu.VMEM((KINDS, size, size), BF),
                 pltpu.VMEM((heads, rows, size), BF),
                 pltpu.VMEM((slots, 2 * nh, rows // nh, size), BF),
-                dma((2,)), dma((nh - 1,)),
-                dma((slots,)), dma((nh - 1,)), dma((slots,)), dma((slots,)),
             ],
             compiler_params=pltpu.CompilerParams(
                 collective_id=0,

time: 43.6 us -> 43.3 us (level)
  no operation moved by 1% of the time
where the time goes in v5:
time: 43.3 us; the launch traced here: 43.1 us
  Pallas kernels  42.1 us (97%)
  local copies, waits for them, and re-layouts  1.06 us (2%)
    pallas_call x1, Pallas kernels, local(): pl.pallas_call(functools.partial(kernel, nh, nz), out_shape=pltpu.VMEM(ou...  42.1 us
    unnamed x1, local copies, waits for them, and re-layouts  1.06 us

profile of v5, /device:TPU:0, one launch (start us, length us, event | category | flops | bytes accessed | tf_op | source)
XLA Modules:
  0.0 43.1 jit_solution(15856303438276387099)
XLA Ops:
  0.0 42.1 %shard_map.73 = bf16[2,64,5120]{2,1,0:T(8,128)(2,1)S(1)} custom-call(bf16[2,256,1280]{2,1,0:T(8,128)(2,1)} %q_in.1, bf16[256,1280]{1,0:T(8,128)(2,1)} %k_in.1, bf16[256,1280]{1,0:T(8,128)(2,1)} %v_in.1, f32[5,256]{1,0:T(8,128)} %r_in.1, f32[5,256,256]{2,1,0:T(8,128)} %g_in.1, f32[5,256,256]{2,1,0:T(8,128)} %u_in.1, f32[5,256,256]{2,1,0:T(8,128)} %d_in.1), custom_call_target="tpu_custom_call" | custom-call | tf_op jit(solution)/shard_map/pallas_call | solution.py:578
  42.1 1.1 %copy.9 = bf16[2,64,5120]{2,1,0:T(8,128)(2,1)} copy(bf16[2,64,5120]{2,1,0:T(8,128)(2,1)S(1)} %shard_map.73) | data formatting | bytes 2621440

commit v6 on v5

--- a/solution.py
+++ b/solution.py
@@ -276,23 +276,25 @@
             return jnp.where(alone & (t >= turn_at), held, t - LAG * far)
 
         def pass_on(t):
-            p = turn(t, z - 1)
-            s = turn(t, nz - 2 - z)
-
-            @pl.when(middle & (p >= 0) & (p < total) & (lax.rem(p, PAIR) == PAIR - 1))
-            def _():
-                n = p // PAIR
-                m, part = place_right(n)
-                right(po, n).wait_recv()
-                po[m, part] = (pi[m, part].astype(F32) + own[m, part].astype(F32)).astype(BF)
-                right(po, n).start()
-
-            @pl.when(middle & (s >= 0) & (s < total))
-            def _():
-                m, part = place(s)
-                left(so, s).wait_recv()
-                so[m, part] = (si[m, part].astype(F32) + own[m, part].astype(F32)).astype(BF)
-                left(so, s).start()
+            @pl.when(middle)
+            def _():
+                p = turn(t, z - 1)
+                s = turn(t, nz - 2 - z)
+
+                @pl.when((p >= 0) & (p < total) & (lax.rem(p, PAIR) == PAIR - 1))
+                def _():
+                    n = p // PAIR
+                    m, part = place_right(n)
+                    right(po, n).wait_recv()
+                    po[m, part] = (pi[m, part].astype(F32) + own[m, part].astype(F32)).astype(BF)
+                    right(po, n).start()
+
+                @pl.when((s >= 0) & (s < total))
+                def _():
+                    m, part = place(s)
+                    left(so, s).wait_recv()
+                    so[m, part] = (si[m, part].astype(F32) + own[m, part].astype(F32)).astype(BF)
+                    left(so, s).start()
 
         def first(h):
             ob[h] = fast_apply(qb[:, cut(h)], wh[1, h], wh[2, h], wh[0, h])
@@ -307,14 +309,16 @@
                 @pl.when(first_end)
                 def _():
                     for g in range(PIECES):
+                        part = pl.ds(g * piece, piece)
                         left(own, per * i + k * PIECES + g).wait_recv()
-                    xs[k] = own[m].astype(F32) + si[m].astype(F32)
+                        xs[k, part] = own[m, part].astype(F32) + si[m, part].astype(F32)
 
                 @pl.when(last_end)
                 def _():
                     for g in range(PIECES // PAIR):
+                        part = pl.ds(g * PAIR * piece, PAIR * piece)
                         right(own, (KINDS * i + k) * (PIECES // PAIR) + g).wait_recv()
-                    xs[k] = own[m].astype(F32) + pi[m].astype(F32)
+                        xs[k, part] = own[m, part].astype(F32) + pi[m, part].astype(F32)
 
                 @pl.when(middle)
                 def _():
@@ -486,9 +490,11 @@
             for item in tail:
                 item()
 
-        @pl.loop(per * (slots + behind), per * slots + LAG_ALONE * hops)
-        def _(t):
-            pass_on(t)
+        @pl.when(middle)
+        def _():
+            @pl.loop(per * (slots + behind), per * slots + LAG_ALONE * hops)
+            def _(t):
+                pass_on(t)
 
         @pl.loop(jnp.where(defer, max(slots - 2, 0), slots - 1), slots)
         def _(i):

time: 43.3 us -> 43.1 us (level)
  no operation moved by 1% of the time
where the time goes in v6:
time: 43.1 us; the launch traced here: 43 us
  Pallas kernels  41.9 us (97%)
  local copies, waits for them, and re-layouts  1.06 us (2%)
    pallas_call x1, Pallas kernels, local(): pl.pallas_call(functools.partial(kernel, nh, nz), out_shape=pltpu.VMEM(ou...  41.9 us
    unnamed x1, local copies, waits for them, and re-layouts  1.06 us

profile of v6, /device:TPU:0, one launch (start us, length us, event | category | flops | bytes accessed | tf_op | source)
XLA Modules:
  0.0 43.0 jit_solution(8310303258332761426)
XLA Ops:
  0.0 41.9 %shard_map.73 = bf16[2,64,5120]{2,1,0:T(8,128)(2,1)S(1)} custom-call(bf16[2,256,1280]{2,1,0:T(8,128)(2,1)} %q_in.1, bf16[256,1280]{1,0:T(8,128)(2,1)} %k_in.1, bf16[256,1280]{1,0:T(8,128)(2,1)} %v_in.1, f32[5,256]{1,0:T(8,128)} %r_in.1, f32[5,256,256]{2,1,0:T(8,128)} %g_in.1, f32[5,256,256]{2,1,0:T(8,128)} %u_in.1, f32[5,256,256]{2,1,0:T(8,128)} %d_in.1), custom_call_target="tpu_custom_call" | custom-call | tf_op jit(solution)/shard_map/pallas_call | solution.py:584
  41.9 1.1 %copy.9 = bf16[2,64,5120]{2,1,0:T(8,128)(2,1)} copy(bf16[2,64,5120]{2,1,0:T(8,128)(2,1)S(1)} %shard_map.73) | data formatting | bytes 2621440

commit v7 on v6

--- a/solution.py
+++ b/solution.py
@@ -12,7 +12,7 @@
 PIECES = 8
 PAIR = 2
 LAG = 10
-LAG_ALONE = 18
+LAG_ALONE = 16
 VMEM_BYTES = 67043328
 
 coef_first = 3.4445

time: 43.1 us -> 43.2 us (level)
  no operation moved by 1% of the time
where the time goes in v7:
time: 43.2 us; the launch traced here: 43.1 us
  Pallas kernels  42 us (97%)
  local copies, waits for them, and re-layouts  1.06 us (2%)
    pallas_call x1, Pallas kernels, local(): pl.pallas_call(functools.partial(kernel, nh, nz), out_shape=pltpu.VMEM(ou...  42 us
    unnamed x1, local copies, waits for them, and re-layouts  1.06 us

profile of v7, /device:TPU:0, one launch (start us, length us, event | category | flops | bytes accessed | tf_op | source)
XLA Modules:
  0.0 43.1 jit_solution(13879184477370061633)
XLA Ops:
  0.0 42.0 %shard_map.73 = bf16[2,64,5120]{2,1,0:T(8,128)(2,1)S(1)} custom-call(bf16[2,256,1280]{2,1,0:T(8,128)(2,1)} %q_in.1, bf16[256,1280]{1,0:T(8,128)(2,1)} %k_in.1, bf16[256,1280]{1,0:T(8,128)(2,1)} %v_in.1, f32[5,256]{1,0:T(8,128)} %r_in.1, f32[5,256,256]{2,1,0:T(8,128)} %g_in.1, f32[5,256,256]{2,1,0:T(8,128)} %u_in.1, f32[5,256,256]{2,1,0:T(8,128)} %d_in.1), custom_call_target="tpu_custom_call" | custom-call | tf_op jit(solution)/shard_map/pallas_call | solution.py:584
  42.0 1.1 %copy.9 = bf16[2,64,5120]{2,1,0:T(8,128)(2,1)} copy(bf16[2,64,5120]{2,1,0:T(8,128)(2,1)S(1)} %shard_map.73) | data formatting | bytes 2621440

commit v8 on v6

--- a/solution.py
+++ b/solution.py
@@ -385,7 +385,7 @@
                 first(h)
 
         first_loads = opening()
-        for copy in first_loads:
+        for copy in (*first_loads[1:3], first_loads[0], *first_loads[3:]):
             copy.start()
 
         @pl.when(z > 0)

time: 43.1 us -> 43.1 us (level)
  no operation moved by 1% of the time
where the time goes in v8:
time: 43.1 us; the launch traced here: 43 us
  Pallas kernels  41.9 us (97%)
  local copies, waits for them, and re-layouts  1.06 us (2%)
    pallas_call x1, Pallas kernels, local(): pl.pallas_call(functools.partial(kernel, nh, nz), out_shape=pltpu.VMEM(ou...  41.9 us
    unnamed x1, local copies, waits for them, and re-layouts  1.06 us

profile of v8, /device:TPU:0, one launch (start us, length us, event | category | flops | bytes accessed | tf_op | source)
XLA Modules:
  0.0 43.0 jit_solution(9720429986717794458)
XLA Ops:
  0.0 41.9 %shard_map.73 = bf16[2,64,5120]{2,1,0:T(8,128)(2,1)S(1)} custom-call(bf16[2,256,1280]{2,1,0:T(8,128)(2,1)} %q_in.1, bf16[256,1280]{1,0:T(8,128)(2,1)} %k_in.1, bf16[256,1280]{1,0:T(8,128)(2,1)} %v_in.1, f32[5,256]{1,0:T(8,128)} %r_in.1, f32[5,256,256]{2,1,0:T(8,128)} %g_in.1, f32[5,256,256]{2,1,0:T(8,128)} %u_in.1, f32[5,256,256]{2,1,0:T(8,128)} %d_in.1), custom_call_target="tpu_custom_call" | custom-call | tf_op jit(solution)/shard_map/pallas_call | solution.py:584
  41.9 1.1 %copy.9 = bf16[2,64,5120]{2,1,0:T(8,128)(2,1)} copy(bf16[2,64,5120]{2,1,0:T(8,128)(2,1)S(1)} %shard_map.73) | data formatting | bytes 2621440
